TPU v7x, 32 devices: a whole 2x2x4 slice. The times are simulated.
32 devices in a mesh: expert: 8 (over z, y), tensor: 4 (over x, core).
Axes of the slice: x: 2, y: 2, z: 4, core: 2. Of those that a mesh axis runs over, the one named last changes fastest.
Arguments:
- tokens: bfloat16 [3152, 768], P('expert'), may hold values from -6 to 6
- norm1_gain: float32 [768], replicated, may hold values from 0.5 to 1.5
- norm1_shift: float32 [768], replicated, may hold values from -4 to 4
- qkv_weight: bfloat16 [768, 2304], P(None, 'tensor'), may hold values from -3 to 3
- proj_weight: bfloat16 [768, 768], P('tensor'), may hold values from -1.75 to 1.75
- proj_shift: float32 [768], replicated, may hold values from -6 to 6
- norm2_gain: float32 [768], replicated, may hold values from 0.5 to 1.5
- norm2_shift: float32 [768], replicated, may hold values from -4 to 4
- router_weight: bfloat16 [768, 8], replicated, may hold values from -8 to 8
- expand_weight: bfloat16 [8, 768, 3072], P('expert', None, 'tensor'), may hold values from -0.21875 to 0.21875
- expand_shift: float32 [8, 3072], P('expert', 'tensor'), may hold values from -6 to 6
- shrink_weight: bfloat16 [8, 3072, 768], P('expert', 'tensor'), may hold values from -0.109375 to 0.109375
- shrink_shift: float32 [8, 768], P('expert'), may hold values from -4 to 4
- route_expert: int32 [3152, 2], P('expert'), may hold values from 0 to 7, as said below
- route_slot: int32 [3152, 2], P('expert'), may hold values from -1 to 123, as said below
- cotangent: bfloat16 [3152, 768], P('expert'), may hold values from -6 to 6
Outputs:
- output: float32 [3152, 768], P('expert')
- tokens_grad: float32 [3152, 768], P('expert')
- gain1_grad: float32 [768], replicated
- shift1_grad: float32 [768], replicated
- qkv_grad: float32 [768, 2304], P(None, 'tensor')
- proj_grad: float32 [768, 768], P('tensor')
- pshift_grad: float32 [768], replicated
- gain2_grad: float32 [768], replicated
- shift2_grad: float32 [768], replicated
- router_grad: float32 [768, 8], replicated
- expand_grad: float32 [8, 768, 3072], P('expert', None, 'tensor')
- eshift_grad: float32 [8, 3072], P('expert', 'tensor')
- shrink_grad: float32 [8, 3072, 768], P('expert', 'tensor')
- sshift_grad: float32 [8, 768], P('expert')
Inputs may be any that keep to these rules, and one draw needn't show every extreme that they name: `route_expert`: each row names two different experts. In some expert's column more than 124 first choices fall in the rows of one device, in every draw. `route_slot`: within the rows of one device and for each expert, the first choices of all rows in row order and then the second choices in row order take slots 0, 1, 2, ... of that expert; once 124 slots are taken, further choices of it get -1. Some expert has all 124 slots taken in every device's rows, in every draw.
All inputs are finite; a program needn't handle non-finite values.
Results may differ from a plain program's by a relative error of at most 0.03.
Values may be sent and summed in bfloat16 or wider, within the bound.
A program may use at most 128 MiB of HBM per device.

v0:
```python
import jax
import jax.numpy as jnp
from jax import lax
from jax.sharding import PartitionSpec as P

DH = 64
SEQ = 197


norm_eps = 1e-06
half_root = 0.7071067811865476
gauss_peak = 0.3989422804014327


def normalize(values, norm_gain, norm_shift):
    row_mean = jnp.mean(values, axis=1, keepdims=True)
    centered = values - row_mean
    variance = jnp.mean(centered * centered, axis=1, keepdims=True)
    inverse = lax.rsqrt(variance + norm_eps)
    scaled = centered * inverse
    return (scaled * norm_gain + norm_shift, scaled, inverse)


def norm_back(upstream, scaled, inverse, norm_gain):
    weighted = upstream * norm_gain
    first_mean = jnp.mean(weighted, axis=1, keepdims=True)
    second_mean = jnp.mean(weighted * scaled, axis=1, keepdims=True)
    return inverse * (weighted - first_mean - scaled * second_mean)


def gelu_exact(preact):
    return 0.5 * preact * (1.0 + lax.erf(preact * half_root))


def gelu_slope(preact):
    return (
        0.5 * (1.0 + lax.erf(preact * half_root))
        + preact * jnp.exp(-0.5 * preact * preact) * gauss_peak
    )


def inner_rows(left_b, right_b):
    return lax.dot_general(
        left_b, right_b, (((0,), (0,)), ((), ())), preferred_element_type=jnp.float32
    )


def outer_cols(left_b, right_b):
    return lax.dot_general(
        left_b, right_b, (((1,), (1,)), ((), ())), preferred_element_type=jnp.float32
    )


def route_tables(route_expert, route_slot, experts, capacity):
    tok_count = route_expert.shape[0]
    kept = route_slot >= 0
    targets = jnp.where(kept, route_expert * capacity + route_slot, experts * capacity).reshape(-1)
    numbers = jnp.arange(2 * tok_count, dtype=jnp.int32)
    owners = (
        jnp.full((experts * capacity,), 2 * tok_count, jnp.int32)
        .at[targets]
        .set(numbers, mode="drop")
    )
    return (targets, owners)


def heads_total(partial_value):
    return lax.psum(partial_value.astype(jnp.bfloat16), "tensor").astype(jnp.float32)


def send_rows(buffer):
    return lax.all_to_all(buffer, "expert", split_axis=0, concat_axis=0, tiled=True)


def return_rows(partial_value, offset):
    summed = lax.psum(partial_value.astype(jnp.bfloat16), "tensor").astype(jnp.float32)
    ready = (summed + offset).astype(jnp.bfloat16)
    return lax.all_to_all(ready, "expert", split_axis=0, concat_axis=0, tiled=True)


def attend_front(normed_b, qkv_weight, images):
    tok_count = normed_b.shape[0]
    head_count = qkv_weight.shape[1] // (3 * DH)
    projected = jnp.dot(normed_b, qkv_weight, preferred_element_type=jnp.float32).astype(
        jnp.bfloat16
    )
    projected = projected.reshape(images, SEQ, head_count, 3, DH)
    queries = projected[:, :, :, 0]
    keys_b = projected[:, :, :, 1]
    values_b = projected[:, :, :, 2]
    scores = jnp.einsum(
        "bqhd,bkhd->bhqk", queries, keys_b, preferred_element_type=jnp.float32
    ) * DH ** (-0.5)
    row_top = jnp.max(scores, axis=3, keepdims=True)
    log_total = row_top + jnp.log(jnp.sum(jnp.exp(scores - row_top), axis=3, keepdims=True))
    attn_b = jnp.exp(scores - log_total).astype(jnp.bfloat16)
    context = jnp.einsum("bhqk,bkhd->bqhd", attn_b, values_b, preferred_element_type=jnp.float32)
    context_b = context.astype(jnp.bfloat16).reshape(tok_count, head_count * DH)
    return (queries, keys_b, values_b, log_total, context_b)


def attend_back(queries, keys_b, values_b, log_total, context_b, context_grad, images):
    tok_count = context_b.shape[0]
    head_count = queries.shape[2]
    factor = DH ** (-0.5)
    scores = (
        jnp.einsum("bqhd,bkhd->bhqk", queries, keys_b, preferred_element_type=jnp.float32) * factor
    )
    attention = jnp.exp(scores - log_total)
    attn_b = attention.astype(jnp.bfloat16)
    grad_ctx = context_grad.reshape(images, SEQ, head_count, DH)
    context_four = context_b.reshape(images, SEQ, head_count, DH)
    value_grad = jnp.einsum("bhqk,bqhd->bkhd", attn_b, grad_ctx, preferred_element_type=jnp.float32)
    attn_grad = jnp.einsum(
        "bqhd,bkhd->bhqk", grad_ctx, values_b, preferred_element_type=jnp.float32
    )
    row_dot = jnp.sum(grad_ctx.astype(jnp.float32) * context_four.astype(jnp.float32), axis=3)
    row_dot = jnp.transpose(row_dot, (0, 2, 1))[:, :, :, None]
    score_grad = (attention * (attn_grad - row_dot) * factor).astype(jnp.bfloat16)
    query_grad = jnp.einsum(
        "bhqk,bkhd->bqhd", score_grad, keys_b, preferred_element_type=jnp.float32
    )
    key_grad = jnp.einsum(
        "bhqk,bqhd->bkhd", score_grad, queries, preferred_element_type=jnp.float32
    )
    stacked = jnp.stack([query_grad, key_grad, value_grad], axis=3)
    return stacked.astype(jnp.bfloat16).reshape(tok_count, head_count * 3 * DH)


def on_device(
    tokens,
    norm1_gain,
    norm1_shift,
    qkv_weight,
    proj_weight,
    proj_shift,
    norm2_gain,
    norm2_shift,
    router_weight,
    expand_weight,
    expand_shift,
    shrink_weight,
    shrink_shift,
    route_expert,
    route_slot,
    cotangent,
):
    experts = lax.axis_size("expert")
    tensor_count = lax.axis_size("tensor")
    tok_count = tokens.shape[0]
    images = tok_count // SEQ
    capacity = tensor_count * (5 * tok_count // (2 * experts * tensor_count) + 1)
    width = tokens.shape[1]
    token_f = tokens.astype(jnp.float32)
    normed, scaled1, inverse1 = normalize(token_f, norm1_gain, norm1_shift)
    normed_b = normed.astype(jnp.bfloat16)
    queries, keys_b, values_b, log_total, context_b = attend_front(normed_b, qkv_weight, images)
    attn_part = jnp.dot(context_b, proj_weight, preferred_element_type=jnp.float32)
    hidden = token_f + heads_total(attn_part) + proj_shift
    normed2, scaled2, inverse2 = normalize(hidden, norm2_gain, norm2_shift)
    mixed_b = normed2.astype(jnp.bfloat16)
    logits = jnp.dot(mixed_b, router_weight, preferred_element_type=jnp.float32)
    pick_mask = (
        lax.broadcasted_iota(jnp.int32, (tok_count, 2, experts), 2) == route_expert[:, :, None]
    ).astype(jnp.float32)
    chosen = jnp.sum(logits[:, None, :] * pick_mask, axis=2)
    gate_top = jnp.max(chosen, axis=1, keepdims=True)
    lifted = jnp.exp(chosen - gate_top)
    gate_weights = lifted / jnp.sum(lifted, axis=1, keepdims=True)
    targets, owners = route_tables(route_expert, route_slot, experts, capacity)
    buffer = jnp.take(mixed_b, owners // 2, axis=0, mode="fill", fill_value=0).reshape(
        experts, capacity, width
    )
    received = send_rows(buffer).reshape(experts * capacity, width)
    preact = (
        jnp.dot(received, expand_weight[0], preferred_element_type=jnp.float32) + expand_shift[0]
    )
    activ_b = gelu_exact(preact).astype(jnp.bfloat16)
    out_part = jnp.dot(activ_b, shrink_weight[0], preferred_element_type=jnp.float32).reshape(
        experts, capacity, width
    )
    returned = return_rows(out_part, shrink_shift[0]).reshape(experts * capacity, width)
    picked = (
        jnp.take(returned, targets, axis=0, mode="fill", fill_value=0)
        .reshape(tok_count, 2, width)
        .astype(jnp.float32)
    )
    output = hidden + jnp.sum(gate_weights[:, :, None] * picked, axis=1)
    upstream = cotangent.astype(jnp.float32)
    gate_grad = jnp.sum(upstream[:, None, :] * picked, axis=2)
    weighted = (
        (gate_weights[:, :, None] * upstream[:, None, :])
        .astype(jnp.bfloat16)
        .reshape(2 * tok_count, width)
    )
    grad_buffer = jnp.take(weighted, owners, axis=0, mode="fill", fill_value=0).reshape(
        experts, capacity, width
    )
    grad_recv = send_rows(grad_buffer).reshape(experts * capacity, width)
    shrink_g = inner_rows(activ_b, grad_recv)
    sshift_g = jnp.sum(grad_recv.astype(jnp.float32), axis=0)
    pre_grad = outer_cols(grad_recv, shrink_weight[0]) * gelu_slope(preact)
    pre_gradb = pre_grad.astype(jnp.bfloat16)
    expand_g = inner_rows(received, pre_gradb)
    eshift_g = jnp.sum(pre_grad, axis=0)
    rows_part = outer_cols(pre_gradb, expand_weight[0]).reshape(experts, capacity, width)
    back_rows = return_rows(rows_part, 0.0).reshape(experts * capacity, width)
    common = jnp.sum(gate_weights * gate_grad, axis=1, keepdims=True)
    chosen_grad = gate_weights * (gate_grad - common)
    logit_grad = jnp.sum(pick_mask * chosen_grad[:, :, None], axis=1).astype(jnp.bfloat16)
    router_g = inner_rows(mixed_b, logit_grad)
    back_pick = (
        jnp.take(back_rows, targets, axis=0, mode="fill", fill_value=0)
        .reshape(tok_count, 2, width)
        .astype(jnp.float32)
    )
    mixed_grad = jnp.sum(back_pick, axis=1) + outer_cols(logit_grad, router_weight)
    gain2_g = jnp.sum(mixed_grad * scaled2, axis=0)
    shift2_g = jnp.sum(mixed_grad, axis=0)
    hidden_grad = upstream + norm_back(mixed_grad, scaled2, inverse2, norm2_gain)
    pshift_g = jnp.sum(hidden_grad, axis=0)
    hidden_gradb = hidden_grad.astype(jnp.bfloat16)
    proj_g = inner_rows(context_b, hidden_gradb)
    context_grad = outer_cols(hidden_gradb, proj_weight).astype(jnp.bfloat16)
    qkv_gradb = attend_back(queries, keys_b, values_b, log_total, context_b, context_grad, images)
    qkv_g = inner_rows(normed_b, qkv_gradb)
    normed_grad = heads_total(outer_cols(qkv_gradb, qkv_weight))
    gain1_g = jnp.sum(normed_grad * scaled1, axis=0)
    shift1_g = jnp.sum(normed_grad, axis=0)
    tokens_grad = hidden_grad + norm_back(normed_grad, scaled1, inverse1, norm1_gain)
    summed = lax.psum(
        (gain1_g, shift1_g, qkv_g, proj_g, pshift_g, gain2_g, shift2_g, router_g), "expert"
    )
    return (
        output,
        tokens_grad,
        summed[0],
        summed[1],
        summed[2],
        summed[3],
        summed[4],
        summed[5],
        summed[6],
        summed[7],
        expand_g[None],
        eshift_g[None],
        shrink_g[None],
        sshift_g[None],
    )


def solution(mesh):
    return jax.shard_map(
        on_device,
        mesh=mesh,
        in_specs=(
            P("expert", None),
            P(),
            P(),
            P(None, "tensor"),
            P("tensor", None),
            P(),
            P(),
            P(),
            P(),
            P("expert", None, "tensor"),
            P("expert", "tensor"),
            P("expert", "tensor", None),
            P("expert", None),
            P("expert", None),
            P("expert", None),
            P("expert", None),
        ),
        out_specs=(
            P("expert", None),
            P("expert", None),
            P(),
            P(),
            P(None, "tensor"),
            P("tensor", None),
            P(),
            P(),
            P(),
            P(),
            P("expert", None, "tensor"),
            P("expert", "tensor"),
            P("expert", "tensor", None),
            P("expert", None),
        ),
        check_vma=False,
    )
```

profile of v0, /device:TPU:20, one launch (start us, length us, event | category | flops | bytes accessed | tf_op | source)
XLA Modules:
  0.0 520.9 jit_solution(4435264701466278154)
XLA Ops:
  10.1 1.9 convolution_convert_fusion.4
  12.0 1.7 reshape.341
  13.7 4.7 fusion.64
  24.1 5.3 %scatter_custom_fusion = s32[992]{0:T(1024)S(1)} fusion(s32[788]{0:T(1024)S(1)} %fusion.54, s32[788]{0:T(1024)S(1)} %iota.9, s32[]{:T(128)} %constant.76.clone.1), kind=kCustom, calls=%fused_computation.127 | custom fusion | bytes 3972 | tf_op jit(solution)/shard_map/scatter | solution.py:62
  29.5 29.2 %all-reduce.8.cloned.1.call-done = bf16[394,768]{1,0:T(8,128)(2,1)} async-done(((bf16[394,768]{1,0:T(8,128)(2,1)}), bf16[394,768]{1,0:T(8,128)(2,1)}) %all-reduce.8.cloned.1.call-update) | async-done | bytes 605200 | tf_op jit(solution)/shard_map/psum | solution.py:68
  60.9 5.2 gather_fusion
  66.1 1.5 gather.16
  69.0 6.4 %all-to-all-start = ((bf16[8,124,768]{2,1,0:T(8,128)(2,1)}), bf16[8,124,768]{2,1,0:T(8,128)(2,1)}, u32[]{:S(2)}, u32[]{:S(2)}) async-start(bf16[8,124,768]{2,1,0:T(8,128)(2,1)} %broadcast_select_fusion.1), calls=%async_computation | async-start | bytes 3145728 | tf_op jit(solution)/shard_map/all_to_all | solution.py:72
  75.5 2.2 mul.221
  77.7 4.1 mul.222
  83.2 1.9 multiply_convert_fusion.1
  85.1 5.2 gather_fusion.1
  93.2 15.0 %all-to-all-done = bf16[8,124,768]{2,1,0:T(8,128)(2,1)} async-done(((bf16[8,124,768]{2,1,0:T(8,128)(2,1)}), bf16[8,124,768]{2,1,0:T(8,128)(2,1)}, u32[]{:S(2)}, u32[]{:S(2)}) %all-to-all-start) | async-done | bytes 1523744 | tf_op jit(solution)/shard_map/all_to_all | solution.py:72
  108.2 7.0 %all-to-all-start.2 = ((bf16[8,124,768]{2,1,0:T(8,128)(2,1)}), bf16[8,124,768]{2,1,0:T(8,128)(2,1)S(1)}, u32[]{:S(2)}, u32[]{:S(2)}) async-start(bf16[8,124,768]{2,1,0:T(8,128)(2,1)} %broadcast_select_fusion), calls=%async_computation.2 | async-start | bytes 3145728 | tf_op jit(solution)/shard_map/all_to_all | solution.py:72
  115.2 2.4 reshape.283
  117.6 4.8 multiply_convert_fusion
  122.5 26.6 %all-to-all-done.2 = bf16[8,124,768]{2,1,0:T(8,128)(2,1)S(1)} async-done(((bf16[8,124,768]{2,1,0:T(8,128)(2,1)}), bf16[8,124,768]{2,1,0:T(8,128)(2,1)S(1)}, u32[]{:S(2)}, u32[]{:S(2)}) %all-to-all-start.2) | async-done | bytes 1523744 | tf_op jit(solution)/shard_map/all_to_all | solution.py:72
  150.7 5.8 %fusion.63 = (f32[768]{0:T(1024)S(1)}, bf16[992,768]{1,0:T(8,128)(2,1)}) fusion(f32[992,768]{1,0:T(8,128)} %get-tuple-element.49, f32[768]{0:T(1024)S(1)} %reduce.3, bf16[992,768]{1,0:T(8,128)(2,1)} %reshape.286, bf16[1,768,768]{2,1,0:T(8,128)(2,1)} %param.29), kind=kOutput, calls=%fused_computation.139 | convolution fusion | flops 1179352320 | bytes 7280640 | tf_op jit(solution)/shard_map/dot_general | solution.py:49
  158.1 2.6 convolution_convert_fusion
  160.7 1.6 dot_general.74
  162.4 2.5 convolution_convert_fusion.1
  165.6 69.4 %all-reduce.14.cloned.1.call-done = (bf16[8,124,768]{2,1,0:T(8,128)(2,1)}, bf16[8,124,768]{2,1,0:T(8,128)(2,1)}) async-done(((bf16[8,124,768]{2,1,0:T(8,128)(2,1)}, bf16[8,124,768]{2,1,0:T(8,128)(2,1)}), (bf16[8,124,768]{2,1,0:T(8,128)(2,1)}, bf16[8,124,768]{2,1,0:T(8,128)(2,1)})) %all-reduce.14.cloned.1.call-update) | async-done | bytes 3047440 | tf_op jit(solution)/shard_map/psum | solution.py:76
  235.0 1.7 add_convert_fusion
  236.7 39.5 %all_to_all.20 = bf16[8,124,768]{2,1,0:T(8,128)(2,1)} all-to-all(bf16[8,124,768]{2,1,0:T(8,128)(2,1)S(1)} %add_convert_fusion), channel_id=1, replica_groups=mesh['expert'=8,'tensor'=4] {'expert'}, dimensions={0} | all-to-all | bytes 3047424 | tf_op jit(solution)/shard_map/all_to_all | solution.py:78
  276.2 7.6 %all-to-all-start.3 = ((bf16[8,124,768]{2,1,0:T(8,128)(2,1)}), bf16[8,124,768]{2,1,0:T(8,128)(2,1)}, u32[]{:S(2)}, u32[]{:S(2)}) async-start(bf16[8,124,768]{2,1,0:T(8,128)(2,1)} %get-tuple-element.32), calls=%async_computation.3 | async-start | bytes 3145728 | tf_op jit(solution)/shard_map/all_to_all | solution.py:78
  283.9 1.5 reshape.284
  285.5 4.0 gather_fusion.2
  289.5 27.0 %all-to-all-done.3 = bf16[8,124,768]{2,1,0:T(8,128)(2,1)} async-done(((bf16[8,124,768]{2,1,0:T(8,128)(2,1)}), bf16[8,124,768]{2,1,0:T(8,128)(2,1)}, u32[]{:S(2)}, u32[]{:S(2)}) %all-to-all-start.3) | async-done | bytes 1523744 | tf_op jit(solution)/shard_map/all_to_all | solution.py:78
  316.5 1.5 reshape.287
  318.0 4.0 gather_fusion.3
  322.1 2.7 multiply_reduce_fusion
  325.2 4.0 select_convert_fusion
  329.1 4.0 reshape.290
  333.1 4.2 reshape.289
  337.4 5.7 %multiply_reduce_fusion.1 = f32[394,768]{1,0:T(8,128)} fusion(f32[394,2,768]{2,1,0:T(2,128)} %reshape.289, f32[394,2]{1,0:T(8,128)S(1)} %copy-done.19), kind=kLoop, calls=%fused_computation.17 | loop fusion | flops 907776 | bytes 3634256 | tf_op jit(solution)/shard_map/reduce_sum | solution.py:188
  343.1 5.7 %reduce_sum.226 = f32[394,768]{1,0:T(8,128)} reduce(f32[394,2,768]{2,1,0:T(2,128)} %reshape.290, f32[]{:T(128)} %constant.48.clone.1), dimensions={1}, to_apply=%region_14.16 | reduce | flops 302592 | bytes 3631108 | tf_op jit(solution)/shard_map/reduce_sum | solution.py:217
  348.8 2.3 multiply_reduce_fusion.2
  351.1 1.7 fusion.62
  358.9 3.0 convolution_convert_fusion.2
  363.4 3.1 fusion.59
  366.5 1.8 convert_reduce_fusion
  369.5 4.4 convolution_bitcast_fusion.1
  373.9 2.9 convolution_bitcast_fusion
  376.9 20.2 %all-reduce.10.cloned.1.call-done = bf16[394,768]{1,0:T(8,128)(2,1)} async-done(((bf16[394,768]{1,0:T(8,128)(2,1)}), bf16[394,768]{1,0:T(8,128)(2,1)}) %all-reduce.10.cloned.1.call-update) | async-done | bytes 605200 | tf_op jit(solution)/shard_map/psum | solution.py:68
  397.2 1.8 fusion.23
  399.0 33.4 %all-reduce = (f32[768]{0:T(1024)}, f32[768]{0:T(1024)}, f32[768]{0:T(1024)}, f32[768]{0:T(1024)}, f32[768]{0:T(1024)}, /*index=5*/f32[768,8]{0,1:T(8,128)}) all-reduce(f32[768]{0:T(1024)S(1)} %get-tuple-element.18, f32[768]{0:T(1024)S(1)} %get-tuple-element.22, ...), channel_id=1, replica_groups=mesh['expert'=8,'tensor'=4] {'expert'}, use_global_device_ids=true, to_apply=%region_25.27 | all-reduce | flops 9984 | bytes 79872 | tf_op jit(solution)/shard_map/psum | solution.py:231
  433.9 76.2 %all-reduce.12.cloned.1.call-done = (f32[768,576]{0,1:T(8,128)}, f32[192,768]{1,0:T(8,128)}) async-done(((f32[768,576]{0,1:T(8,128)}, f32[192,768]{1,0:T(8,128)}), (f32[768,576]{0,1:T(8,128)}, f32[192,768]{1,0:T(8,128)})) %all-reduce.12.cloned.1.call-update) | async-done | bytes 2359312 | tf_op jit(solution)/shard_map/psum | solution.py:231
  510.1 2.9 copy.99
  (174 shorter events, 32.0 us)
Async XLA Ops:
  7.2 110.5 %copy-start = (bf16[1,768,768]{2,1,0:T(8,128)(2,1)S(1)}, bf16[1,768,768]{2,1,0:T(8,128)(2,1)}, u32[]{:S(2)}) copy-start(bf16[1,768,768]{2,1,0:T(8,128)(2,1)} %param.27) | copy-start | bytes 3538948
  7.2 2.8 copy-start.2
  7.2 2.8 copy-start.39
  7.2 2.8 copy-start.46
  7.2 51.5 %all-reduce.8.cloned.1.call-start = ((), (), s32[]{:S(2)}) async-start(), calls=%async_computation.4 | async-start | bytes 1228800 | tf_op jit(solution)/shard_map/psum | solution.py:68
  19.7 1.3 copy-start.24
  20.2 1.1 copy-start.20
  21.3 1.2 copy-start.33
  22.1 1.6 copy-start.22
  22.1 1.6 copy-start.37
  22.1 1.6 copy-start.42
  22.3 36.4 %copy-start.36 = (f32[768]{0:T(1024)S(1)}, f32[768]{0:T(1024)}, u32[]{:S(2)}) copy-start(f32[768]{0:T(1024)} %param.23) | copy-start | bytes 9220
  22.5 1.2 copy-start.28
  23.9 36.6 %copy-start.16 = (s32[394,2]{1,0:T(8,128)}, s32[394,2]{1,0:T(8,128)S(1)}, u32[]{:S(2)}) copy-start(s32[394,2]{1,0:T(8,128)S(1)} %copy.65) | copy-start | bytes 9460
  29.5 31.0 %copy-start.38 = (f32[768]{0:T(1024)S(1)}, f32[768]{0:T(1024)}, u32[]{:S(2)}) copy-start(f32[768]{0:T(1024)} %param.24) | copy-start | bytes 9220
  29.5 31.0 %copy-start.41 = (f32[768]{0:T(1024)S(1)}, f32[768]{0:T(1024)}, u32[]{:S(2)}) copy-start(f32[768]{0:T(1024)} %param.25) | copy-start | bytes 9220
  58.7 1.4 copy-start.10
  69.0 6.5 %copy-start.13 = (bf16[394,768]{1,0:T(8,128)(2,1)S(1)}, bf16[394,768]{1,0:T(8,128)(2,1)}, u32[]{:S(2)}) copy-start(bf16[394,768]{1,0:T(8,128)(2,1)} %param.33) | copy-start | bytes 1815556
  69.0 39.2 %all-to-all-start = ((bf16[8,124,768]{2,1,0:T(8,128)(2,1)}), bf16[8,124,768]{2,1,0:T(8,128)(2,1)}, u32[]{:S(2)}, u32[]{:S(2)}) async-start(bf16[8,124,768]{2,1,0:T(8,128)(2,1)} %broadcast_select_fusion.1), calls=%async_computation | async-start | bytes 3145728 | tf_op jit(solution)/shard_map/all_to_all | solution.py:72
  77.7 4.1 copy-start.40
  93.1 22.0 %copy-start.43 = (f32[1,768]{1,0:T(1,128)S(1)}, f32[1,768]{1,0:T(1,128)}, u32[]{:S(2)}) copy-start(f32[1,768]{1,0:T(1,128)} %param.28) | copy-start | bytes 9220
  108.2 40.9 %all-to-all-start.2 = ((bf16[8,124,768]{2,1,0:T(8,128)(2,1)}), bf16[8,124,768]{2,1,0:T(8,128)(2,1)S(1)}, u32[]{:S(2)}, u32[]{:S(2)}) async-start(bf16[8,124,768]{2,1,0:T(8,128)(2,1)} %broadcast_select_fusion), calls=%async_computation.2 | async-start | bytes 3145728 | tf_op jit(solution)/shard_map/all_to_all | solution.py:72
  115.2 119.9 %all-reduce.14.cloned.1.call-start = ((), (), s32[]{:S(2)}) async-start(), calls=%async_computation.7 | async-start | bytes 6291456 | tf_op jit(solution)/shard_map/psum | solution.py:76
  149.1 1.6 copy-start.8
  160.7 1.7 copy-start.45
  276.2 7.6 %copy-start.17 = (s32[394,2]{1,0:T(8,128)S(1)}, s32[394,2]{1,0:T(8,128)}, u32[]{:S(2)}) copy-start(s32[394,2]{1,0:T(8,128)} %copy-done.16) | copy-start | bytes 9460
  276.2 40.3 %all-to-all-start.3 = ((bf16[8,124,768]{2,1,0:T(8,128)(2,1)}), bf16[8,124,768]{2,1,0:T(8,128)(2,1)}, u32[]{:S(2)}, u32[]{:S(2)}) async-start(bf16[8,124,768]{2,1,0:T(8,128)(2,1)} %get-tuple-element.32), calls=%async_computation.3 | async-start | bytes 3145728 | tf_op jit(solution)/shard_map/all_to_all | solution.py:78
  283.7 113.4 %all-reduce.10.cloned.1.call-start = ((), (), s32[]{:S(2)}) async-start(), calls=%async_computation.5 | async-start | bytes 1228800 | tf_op jit(solution)/shard_map/psum | solution.py:68
  322.1 3.1 copy-start.9
  333.1 4.2 copy-start.19
  343.1 5.7 %copy-start.3 = (bf16[394,768]{1,0:T(8,128)(2,1)S(1)}, bf16[394,768]{1,0:T(8,128)(2,1)}, u32[]{:S(2)}) copy-start(bf16[394,768]{1,0:T(8,128)(2,1)} %param.18) | copy-start | bytes 1815556
  343.1 5.7 %copy-start.11 = (bf16[394,768]{1,0:T(8,128)(2,1)S(1)}, bf16[394,768]{1,0:T(8,128)(2,1)}, u32[]{:S(2)}) copy-start(bf16[394,768]{1,0:T(8,128)(2,1)} %all-reduce.8.cloned.1.call-done) | copy-start | bytes 1815556
  348.8 2.3 copy-start.12
  348.8 2.3 copy-start.14
  351.1 2.8 copy-start.34
  352.8 1.6 copy-start.23
  353.9 1.3 copy-start.5
  354.3 1.3 copy-start.21
  355.5 1.2 copy-start.27
  358.9 3.3 copy-start.7
  358.9 3.3 copy-start.29
  361.9 148.2 %all-reduce.12.cloned.1.call-start = ((), (), s32[]{:S(2)}) async-start(), calls=%async_computation.6 | async-start | bytes 4718592 | tf_op jit(solution)/shard_map/psum | solution.py:231
  366.5 3.0 copy-start.30
  369.5 4.4 copy-start.31
  369.5 4.4 copy-start.32
  397.2 35.2 %copy-start.15 = (bf16[394,768]{1,0:T(8,128)(2,1)S(1)}, bf16[394,768]{1,0:T(8,128)(2,1)}, u32[]{:S(2)}) copy-start(bf16[394,768]{1,0:T(8,128)(2,1)} %all-reduce.10.cloned.1.call-done) | copy-start | bytes 1815556
  510.1 2.9 copy-start.35
  510.1 3.7 copy-start.1
  (6 other events, 5.1 us)
Sparse Core Ops, SparseCore 0:
  23.8 34.8 all-reduce.7
  165.1 69.8 all-reduce.13
  362.1 35.0 all-reduce.9
  401.2 108.9 all-reduce.11
where the time goes:
time: 531 us; the launch traced here: 521 us
  waiting for transfers between devices  264 us (50%)
  blocking collectives  72.9 us (14%)
  local copies, waits for them, and re-layouts  72.7 us (14%)
  matrix products  38.5 us (7%)
  other arithmetic  36.8 us (7%)
  starting transfers between devices  21.3 us (4%)
  between operations  14.9 us (3%)
    psum x1, waiting for transfers between devices, on_device(): lax.psum((gain1_g, shift1_g, qkv_g, proj_g, pshift_g, gain2_g, shift2_g,...  76.2 us
    psum x1, waiting for transfers between devices, return_rows(): lax.psum(partial_value.astype(jnp.bfloat16), 'tensor').astype(jnp.float32)  69.4 us
    psum x2, waiting for transfers between devices, heads_total(): lax.psum(partial_value.astype(jnp.bfloat16), 'tensor').astype(jnp.float32)  49.4 us
    all_to_all x2, waiting for transfers between devices, send_rows(): lax.all_to_all(buffer, 'expert', split_axis=0, concat_axis=0, tiled=True)  41.6 us
    all_to_all x1, blocking collectives, return_rows(): lax.all_to_all(ready, 'expert', split_axis=0, concat_axis=0, tiled=True)  39.5 us
    psum x1, blocking collectives, on_device(): lax.psum((gain1_g, shift1_g, qkv_g, proj_g, pshift_g, gain2_g, shift2_g,...  33.4 us
    all_to_all x1, waiting for transfers between devices, return_rows(): lax.all_to_all(ready, 'expert', split_axis=0, concat_axis=0, tiled=True)  27 us
    dot_general x5, matrix products, outer_cols(): lax.dot_general(left_b, right_b, (((1,), (1,)), ((), ())), preferred_elem...  14.1 us
  transfers between devices with their start and end apart: 7, of which 7 were waited for; matrix products, arithmetic and copies ran while one was open for 10% of the time, Pallas kernels for 0%

commit v1 on v0

--- a/solution.py
+++ b/solution.py
@@ -1,6 +1,8 @@
 import jax
 import jax.numpy as jnp
 from jax import lax
+from jax.experimental import pallas as pl
+from jax.experimental.pallas import tpu as pltpu
 from jax.sharding import PartitionSpec as P
 
 DH = 64
@@ -127,7 +129,7 @@
     return stacked.astype(jnp.bfloat16).reshape(tok_count, head_count * 3 * DH)
 
 
-def on_device(
+def plain_device(
     tokens,
     norm1_gain,
     norm1_shift,
@@ -248,8 +250,513 @@
         sshift_g[None],
     )
 
+MESH = pl.DeviceIdType.MESH
+F32 = jnp.float32
+BF16 = jnp.bfloat16
+
+
+def place():
+    e = lax.axis_index("expert")
+    t = lax.axis_index("tensor")
+    a = t // 2
+    c = t % 2
+    return e, t, a, c, (e, 2 * a + 1 - c), (e, 2 * (1 - a) + c)
+
+
+def greet(devices):
+    barrier = pltpu.get_barrier_semaphore()
+    for device in devices:
+        pl.semaphore_signal(barrier, inc=1, device_id=device, device_id_type=MESH)
+    pl.semaphore_wait(barrier, len(devices))
+
+
+def remote(src, dst, send, recv, device):
+    return pltpu.make_async_remote_copy(
+        src_ref=src, dst_ref=dst, send_sem=send, recv_sem=recv, device_id=device, device_id_type=MESH
+    )
+
+
+def lanes(index, width):
+    return pl.ds(pl.multiple_of(index * width, 128), width)
+
+
+def call(kernel, outs, scratch, number, args):
+    vmem = pl.BlockSpec(memory_space=pltpu.VMEM)
+    return pl.pallas_call(
+        kernel,
+        out_shape=outs,
+        in_specs=[vmem] * len(args),
+        out_specs=jax.tree.map(lambda _: vmem, outs),
+        scratch_shapes=scratch,
+        compiler_params=pltpu.CompilerParams(
+            collective_id=number, has_side_effects=True, vmem_limit_bytes=48 * 1024 * 1024
+        ),
+    )(*args)
+
+
+def tensor_sum_kernel(x, out, got1, part, got2, send, recv):
+    e, t, a, c, core, across = place()
+    greet([core, across])
+    half = x.shape[1] // 2
+    mine, other = lanes(c, half), lanes(1 - c, half)
+    copy = remote(x.at[:, other], got1, send.at[0], recv.at[0], core)
+    copy.start()
+    copy.wait()
+    part[...] = (x[:, mine].astype(F32) + got1[...].astype(F32)).astype(BF16)
+    copy = remote(part, got2, send.at[1], recv.at[1], across)
+    copy.start()
+    copy.wait()
+    out[:, mine] = (part[...].astype(F32) + got2[...].astype(F32)).astype(BF16)
+    copy = remote(out.at[:, mine], out.at[:, mine], send.at[2], recv.at[2], core)
+    copy.start()
+    copy.wait()
+
+
+def tensor_sum(x, number):
+    rows, width = x.shape
+    half = pltpu.VMEM((rows, width // 2), BF16)
+    sems = pltpu.SemaphoreType.DMA((3,))
+    return call(
+        tensor_sum_kernel,
+        jax.ShapeDtypeStruct((rows, width), BF16),
+        [half, half, half, sems, sems],
+        number,
+        (x,),
+    )
+
+
+def dispatch_kernel(first, second, out0, out1, send_far, send_across, send_core, recv, local):
+    e, t, a, c, core, across = place()
+    count = first.shape[0]
+    peers = [(lax.rem(e + d, count), t) for d in range(1, count)]
+    greet(peers + [core, across])
+    ins, outs = (first, second), (out0, out1)
+    sent = []
+
+    def push(src, k, origin, quarter, send, device):
+        copy = remote(src, outs[k].at[origin, quarter], send, recv.at[k, origin, quarter], device)
+        copy.start()
+        sent.append(copy)
+
+    def arrive(k, origin, quarter):
+        spot = outs[k].at[origin, quarter]
+        remote(spot, spot, send_core.at[k, origin, quarter], recv.at[k, origin, quarter], core).wait_recv()
+
+    for d in range(1, count):
+        dst = lax.rem(e + d, count)
+        for k in range(2):
+            push(ins[k].at[dst], k, e, t, send_far.at[k, d], (dst, t))
+    keeps = []
+    for k in range(2):
+        push(ins[k].at[e], k, e, t, send_across.at[k, e], across)
+        push(ins[k].at[e], k, e, t, send_core.at[k, e, t], core)
+        keep = pltpu.make_async_copy(ins[k].at[e], outs[k].at[e, t], local.at[k])
+        keep.start()
+        keeps.append(keep)
+    far = 2 * (1 - a) + c
+    for d in range(1, count + 1):
+        if d < count:
+            origin = lax.rem(e - d + count, count)
+            for k in range(2):
+                arrive(k, origin, t)
+                push(outs[k].at[origin, t], k, origin, t, send_across.at[k, origin], across)
+                push(outs[k].at[origin, t], k, origin, t, send_core.at[k, origin, t], core)
+        origin = lax.rem(e - d + 1 + count, count)
+        for k in range(2):
+            arrive(k, origin, far)
+            push(outs[k].at[origin, far], k, origin, far, send_core.at[k, origin, far], core)
+    for d in range(count):
+        origin = lax.rem(e - d + count, count)
+        for k in range(2):
+            arrive(k, origin, 2 * a + 1 - c)
+            arrive(k, origin, 2 * (1 - a) + 1 - c)
+    for copy in sent:
+        copy.wait_send()
+    for keep in keeps:
+        keep.wait()
+
+
+def dispatch(first, second, number):
+    count, rows, width = first.shape
+    out = jax.ShapeDtypeStruct((count, 4, rows, width), BF16)
+    dma = pltpu.SemaphoreType.DMA
+    return call(
+        dispatch_kernel,
+        (out, out),
+        [dma((2, count)), dma((2, count)), dma((2, count, 4)), dma((2, count, 4)), dma((2,))],
+        number,
+        (first, second),
+    )
+
+
+def collect_kernel(
+    part0, part1, shift, out0, out1, got1, half1, got2, ready,
+    send1, recv1, send2, recv2, send3, recv3, send4, recv4, local,
+):
+    e, t, a, c, core, across = place()
+    count = part0.shape[0]
+    peers = [(lax.rem(e + d, count), t) for d in range(1, count)]
+    greet(peers + [core, across])
+    parts, outs = (part0, part1), (out0, out1)
+    rows = part0.shape[1] // 2
+    width = part0.shape[2] // 2
+    mine, other = pl.ds(c * rows, rows), pl.ds((1 - c) * rows, rows)
+    left, right = lanes(a, width), lanes(1 - a, width)
+    order = [lax.rem(e + d, count) for d in range(1, count + 1)]
+    steps = [(dst, k) for dst in order for k in range(2)]
+    stage1, stage2, rest = [], [], []
+    for dst, k in steps:
+        copy = remote(parts[k].at[dst, other], got1.at[k, dst], send1.at[k, dst], recv1.at[k, dst], core)
+        copy.start()
+        stage1.append(copy)
+    for i, (dst, k) in enumerate(steps):
+        stage1[i].wait_recv()
+        half1[k, dst] = (parts[k][dst, mine].astype(F32) + got1[k, dst].astype(F32)).astype(BF16)
+        copy = remote(
+            half1.at[k, dst, :, right], got2.at[k, dst], send2.at[k, dst], recv2.at[k, dst], across
+        )
+        copy.start()
+        stage2.append(copy)
+    keeps = []
+    for i, (dst, k) in enumerate(steps):
+        stage2[i].wait_recv()
+        total = half1[k, dst, :, left].astype(F32) + got2[k, dst].astype(F32)
+        if k == 0:
+            total = total + shift[:, left]
+        ready[k, dst] = total.astype(BF16)
+        if i < len(steps) - 2:
+            copy = remote(ready.at[k, dst], outs[k].at[e, c], send3.at[k, dst], recv3.at[k, e], (dst, t))
+            copy.start()
+            rest.append(copy)
+        else:
+            copy = remote(ready.at[k, dst], outs[k].at[e, c], send4.at[k, e], recv4.at[k, e], core)
+            copy.start()
+            rest.append(copy)
+            keep = pltpu.make_async_copy(ready.at[k, dst], outs[k].at[e, c], local.at[k])
+            keep.start()
+            keeps.append(keep)
+    for d in range(1, count):
+        origin = lax.rem(e - d + count, count)
+        for k in range(2):
+            spot = outs[k].at[origin, c]
+            remote(spot, spot, send4.at[k, origin], recv3.at[k, origin], core).wait_recv()
+            copy = remote(spot, spot, send4.at[k, origin], recv4.at[k, origin], core)
+            copy.start()
+            rest.append(copy)
+    for d in range(count):
+        origin = lax.rem(e - d + count, count)
+        for k in range(2):
+            spot = outs[k].at[origin, 1 - c]
+            remote(spot, spot, send4.at[k, origin], recv4.at[k, origin], core).wait_recv()
+    for copy in stage1 + stage2 + rest:
+        copy.wait_send()
+    for keep in keeps:
+        keep.wait()
+
+
+def collect(part0, part1, shift, number):
+    count, rows, width = part0.shape
+    out = jax.ShapeDtypeStruct((count, 2, rows // 2, width // 2), BF16)
+    dma = pltpu.SemaphoreType.DMA
+    full = pltpu.VMEM((2, count, rows // 2, width), BF16)
+    half = pltpu.VMEM((2, count, rows // 2, width // 2), BF16)
+    return call(
+        collect_kernel,
+        (out, out),
+        [full, full, half, half] + [dma((2, count))] * 8 + [dma((2,))],
+        number,
+        (part0, part1, shift),
+    )
+
+
+def swap_kernel(first, second, gate, out0, out1, gate_out, got, send, recv, send_gate, recv_gate):
+    e, t, a, c, core, across = place()
+    greet([core, across])
+    width = first.shape[1]
+    mine, other = lanes(a, width), lanes(1 - a, width)
+    small = remote(gate, got, send_gate, recv_gate, across)
+    small.start()
+
+    def trade(src, out, out_other):
+        out_here = out.at[:, mine]
+        copy = remote(src, out_here, send.at[0], recv.at[0], across)
+        copy.start()
+        out0[:, mine] = first[...]
+        out1[:, mine] = second[...]
+        copy.wait()
+        spot = out.at[:, other]
+        copy = remote(spot, spot, send.at[1], recv.at[1], core)
+        copy.start()
+        spot_other = out_other.at[:, other]
+        remote(spot_other, spot_other, send.at[1], recv.at[1], core).wait_recv()
+        copy.wait_send()
+
+    @pl.when(c == 0)
+    def _():
+        trade(first, out0, out1)
+
+    @pl.when(c == 1)
+    def _():
+        trade(second, out1, out0)
+
+    small.wait()
+    gate_out[...] = gate[...] + got[...]
+
+
+def swap(first, second, gate, number):
+    rows, width = first.shape
+    out = jax.ShapeDtypeStruct((rows, 2 * width), BF16)
+    dma = pltpu.SemaphoreType.DMA
+    return call(
+        swap_kernel,
+        (out, out, jax.ShapeDtypeStruct(gate.shape, F32)),
+        [pltpu.VMEM(gate.shape, F32), dma((2,)), dma((2,)), dma(()), dma(())],
+        number,
+        (first, second, gate),
+    )
+
+
+def expert_sum_kernel(
+    big, small, out, out_small, got1, sgot1, half1, shalf1, got2, sgot2,
+    send1, recv1, send2, recv2, send3, recv3, send4, recv4,
+):
+    e, t, a, c, core, across = place()
+    z = e // 2
+    y = e % 2
+    deep = big.shape[0] // 2
+    beside = (2 * z + 1 - y, t)
+    greet([beside] + [(2 * lax.rem(z + d, deep) + y, t) for d in range(1, deep)])
+    stage1, stage2, rest = [], [], []
+    order = [2, 1, 3, 0]
+    for d in order:
+        zz = lax.rem(z + d, deep)
+        chunk = 2 * zz + 1 - y
+        pair = (
+            remote(big.at[chunk], got1.at[zz], send1.at[0, zz], recv1.at[0, zz], beside),
+            remote(small.at[chunk], sgot1.at[zz], send1.at[1, zz], recv1.at[1, zz], beside),
+        )
+        for copy in pair:
+            copy.start()
+        stage1.append(pair)
+    for i, d in enumerate(order):
+        zz = lax.rem(z + d, deep)
+        chunk = 2 * zz + y
+        for copy in stage1[i]:
+            copy.wait_recv()
+        half1[zz] = (big[chunk].astype(F32) + got1[zz].astype(F32)).astype(BF16)
+        shalf1[zz] = small[chunk] + sgot1[zz]
+        if d:
+            for copy in (
+                remote(half1.at[zz], got2.at[z], send2.at[0, zz], recv2.at[0, z], (chunk, t)),
+                remote(shalf1.at[zz], sgot2.at[z], send2.at[1, zz], recv2.at[1, z], (chunk, t)),
+            ):
+                copy.start()
+                rest.append(copy)
+    total = half1[z].astype(F32)
+    stotal = shalf1[z]
+    for d in (3, 1, 2):
+        zz = lax.rem(z + d, deep)
+        spot, sspot = got2.at[zz], sgot2.at[zz]
+        remote(spot, spot, send2.at[0, zz], recv2.at[0, zz], beside).wait_recv()
+        remote(sspot, sspot, send2.at[1, zz], recv2.at[1, zz], beside).wait_recv()
+        total = total + got2[zz].astype(F32)
+        stotal = stotal + sgot2[zz]
+    out[e] = total.astype(BF16)
+    out_small[e] = stotal
+    both = (out, out_small)
+    for d in (2, 1, 3):
+        zz = lax.rem(z + d, deep)
+        for k in range(2):
+            spot = both[k].at[e]
+            copy = remote(spot, spot, send3.at[k, zz], recv3.at[k, z], (2 * zz + y, t))
+            copy.start()
+            rest.append(copy)
+    for d in (0, 3, 1, 2):
+        zz = lax.rem(z + d, deep)
+        for k in range(2):
+            spot = both[k].at[2 * zz + y]
+            if d:
+                remote(spot, spot, send4.at[k, zz], recv3.at[k, zz], beside).wait_recv()
+            copy = remote(spot, spot, send4.at[k, zz], recv4.at[k, zz], beside)
+            copy.start()
+            rest.append(copy)
+    for zz in range(deep):
+        for k in range(2):
+            spot = both[k].at[2 * zz + 1 - y]
+            remote(spot, spot, send4.at[k, zz], recv4.at[k, zz], beside).wait_recv()
+    for pair in stage1:
+        for copy in pair:
+            copy.wait_send()
+    for copy in rest:
+        copy.wait_send()
+
+
+def expert_sum(big, small, number):
+    count, rows, width = big.shape
+    deep = count // 2
+    dma = pltpu.SemaphoreType.DMA
+    large = pltpu.VMEM((deep, rows, width), BF16)
+    little = pltpu.VMEM((deep,) + small.shape[1:], F32)
+    return call(
+        expert_sum_kernel,
+        (jax.ShapeDtypeStruct(big.shape, BF16), jax.ShapeDtypeStruct(small.shape, F32)),
+        [large, little, large, little, large, little] + [dma((2, deep))] * 8,
+        number,
+        (big, small),
+    )
+
+
+def fast_device(
+    tokens,
+    norm1_gain,
+    norm1_shift,
+    qkv_weight,
+    proj_weight,
+    proj_shift,
+    norm2_gain,
+    norm2_shift,
+    router_weight,
+    expand_weight,
+    expand_shift,
+    shrink_weight,
+    shrink_shift,
+    route_expert,
+    route_slot,
+    cotangent,
+):
+    experts = lax.axis_size("expert")
+    tensor_count = lax.axis_size("tensor")
+    tensor_index = lax.axis_index("tensor")
+    tok_count = tokens.shape[0]
+    images = tok_count // SEQ
+    capacity = tensor_count * (5 * tok_count // (2 * experts * tensor_count) + 1)
+    quarter = -(-capacity // (16 * tensor_count)) * 16
+    padded = quarter * tensor_count
+    width = tokens.shape[1]
+    half = width // 2
+    token_f = tokens.astype(F32)
+    normed, scaled1, inverse1 = normalize(token_f, norm1_gain, norm1_shift)
+    normed_b = normed.astype(BF16)
+    queries, keys_b, values_b, log_total, context_b = attend_front(normed_b, qkv_weight, images)
+    attn_part = jnp.dot(context_b, proj_weight, preferred_element_type=F32).astype(BF16)
+    hidden = token_f + tensor_sum(attn_part, 1).astype(F32) + proj_shift
+    normed2, scaled2, inverse2 = normalize(hidden, norm2_gain, norm2_shift)
+    mixed_b = normed2.astype(BF16)
+    logits = jnp.dot(mixed_b, router_weight, preferred_element_type=F32)
+    picks = [
+        lax.broadcasted_iota(jnp.int32, (tok_count, experts), 1) == route_expert[:, j : j + 1]
+        for j in range(2)
+    ]
+    chosen = [jnp.sum(jnp.where(pick, logits, 0.0), axis=1, keepdims=True) for pick in picks]
+    gate_top = jnp.maximum(chosen[0], chosen[1])
+    lifted = [jnp.exp(value - gate_top) for value in chosen]
+    gates = [value / (lifted[0] + lifted[1]) for value in lifted]
+    spots = jnp.where(route_slot >= 0, route_expert * padded + route_slot, -1)
+    spots_t = spots.T
+    row_ids = lax.broadcasted_iota(jnp.int32, (experts, quarter, 1), 0) * padded
+    row_ids = row_ids + lax.broadcasted_iota(jnp.int32, (experts, quarter, 1), 1)
+    row_ids = (row_ids + tensor_index * quarter).reshape(experts * quarter, 1)
+    hits = [row_ids == spots_t[j][None, :] for j in range(2)]
+    chooser = (hits[0] | hits[1]).astype(BF16)
+    slot_gate = jnp.sum(
+        jnp.where(hits[0], gates[0].reshape(1, -1), 0.0)
+        + jnp.where(hits[1], gates[1].reshape(1, -1), 0.0),
+        axis=1,
+        keepdims=True,
+    )
+    rows_out = jnp.dot(chooser, mixed_b, preferred_element_type=F32).astype(BF16)
+    grad_out = (slot_gate * jnp.dot(chooser, cotangent, preferred_element_type=F32)).astype(BF16)
+    received, grad_recv = dispatch(
+        rows_out.reshape(experts, quarter, width), grad_out.reshape(experts, quarter, width), 2
+    )
+    received = received.reshape(experts * padded, width)
+    grad_recv = grad_recv.reshape(experts * padded, width)
+    preact = jnp.dot(received, expand_weight[0], preferred_element_type=F32) + expand_shift[0]
+    activ_b = gelu_exact(preact).astype(BF16)
+    out_part = jnp.dot(activ_b, shrink_weight[0], preferred_element_type=F32).astype(BF16)
+    pre_grad = outer_cols(grad_recv, shrink_weight[0]) * gelu_slope(preact)
+    pre_gradb = pre_grad.astype(BF16)
+    rows_part = outer_cols(pre_gradb, expand_weight[0]).astype(BF16)
+    returned, back_rows = collect(
+        out_part.reshape(experts, padded, width),
+        rows_part.reshape(experts, padded, width),
+        shrink_shift,
+        3,
+    )
+    returned = returned.reshape(experts * padded, half)
+    back_rows = back_rows.reshape(experts * padded, half)
+    shrink_g = inner_rows(activ_b, grad_recv)
+    sshift_g = jnp.sum(grad_recv.astype(F32), axis=0)
+    expand_g = inner_rows(received, pre_gradb)
+    eshift_g = jnp.sum(pre_grad, axis=0)
+    upstream = cotangent.astype(F32)
+    slots = lax.broadcasted_iota(jnp.int32, (tok_count, experts * padded), 1)
+    marks = [slots == spots[:, j : j + 1] for j in range(2)]
+    mixer = (jnp.where(marks[0], gates[0], 0.0) + jnp.where(marks[1], gates[1], 0.0)).astype(BF16)
+    gather = (marks[0] | marks[1]).astype(BF16)
+    added = jnp.dot(mixer, returned, preferred_element_type=F32).astype(BF16)
+    back = jnp.dot(gather, back_rows, preferred_element_type=F32).astype(BF16)
+    cot_half = lax.dynamic_slice(cotangent, (0, (tensor_index // 2) * half), (tok_count, half))
+    dots = outer_cols(cot_half, returned)
+    gate_part = jnp.stack([jnp.sum(jnp.where(mark, dots, 0.0), axis=1) for mark in marks])
+    gate_part = jnp.pad(gate_part, ((0, 6), (0, -tok_count % 128)))
+    added, back, gate_full = swap(added, back, gate_part, 4)
+    output = hidden + added.astype(F32)
+    gate_grad = [gate_full[j, :tok_count].reshape(tok_count, 1) for j in range(2)]
+    common = gates[0] * gate_grad[0] + gates[1] * gate_grad[1]
+    logit_grad = (
+        jnp.where(picks[0], gates[0] * (gate_grad[0] - common), 0.0)
+        + jnp.where(picks[1], gates[1] * (gate_grad[1] - common), 0.0)
+    ).astype(BF16)
+    router_g = inner_rows(logit_grad, mixed_b)
+    mixed_grad = back.astype(F32) + outer_cols(logit_grad, router_weight)
+    gain2_g = jnp.sum(mixed_grad * scaled2, axis=0)
+    shift2_g = jnp.sum(mixed_grad, axis=0)
+    hidden_grad = upstream + norm_back(mixed_grad, scaled2, inverse2, norm2_gain)
+    pshift_g = jnp.sum(hidden_grad, axis=0)
+    hidden_gradb = hidden_grad.astype(BF16)
+    context_grad = outer_cols(hidden_gradb, proj_weight).astype(BF16)
+    qkv_gradb = attend_back(queries, keys_b, values_b, log_total, context_b, context_grad, images)
+    normed_grad = tensor_sum(outer_cols(qkv_gradb, qkv_weight).astype(BF16), 5).astype(F32)
+    gain1_g = jnp.sum(normed_grad * scaled1, axis=0)
+    shift1_g = jnp.sum(normed_grad, axis=0)
+    tokens_grad = hidden_grad + norm_back(normed_grad, scaled1, inverse1, norm1_gain)
+    qkv_g = inner_rows(normed_b, qkv_gradb)
+    proj_g = inner_rows(hidden_gradb, context_b)
+    big = jnp.concatenate([qkv_g.astype(BF16), proj_g.astype(BF16)], axis=1)
+    wide = big.shape[1]
+    small = jnp.concatenate(
+        [jnp.stack([gain1_g, shift1_g, pshift_g, gain2_g, shift2_g]), router_g], axis=0
+    )
+    names = small.shape[0]
+    piece = width // experts
+    small = jnp.pad(small, ((0, -names % 8), (0, 0)))
+    small = small.reshape(small.shape[0], experts, piece).transpose(1, 0, 2)
+    small = jnp.pad(small, ((0, 0), (0, 0), (0, -piece % 128)))
+    big, small = expert_sum(big.reshape(experts, piece, wide), small, 6)
+    big = big.reshape(width, wide)
+    small = small[:, :, :piece].transpose(1, 0, 2).reshape(-1, width)
+    return (
+        output,
+        tokens_grad,
+        small[0],
+        small[1],
+        big[:, : qkv_g.shape[1]].astype(F32),
+        big[:, qkv_g.shape[1] :].T.astype(F32),
+        small[2],
+        small[3],
+        small[4],
+        small[5:names].T,
+        expand_g[None],
+        eshift_g[None],
+        shrink_g[None],
+        sshift_g[None],
+    )
+
 
 def solution(mesh):
+    small_mesh = mesh.shape["expert"] == 8 and mesh.shape["tensor"] == 4
+    on_device = fast_device if small_mesh else plain_device
     return jax.shard_map(
         on_device,
         mesh=mesh,

time: 531 us -> 219 us (0.41); the launches traced: 521 us -> 218 us
  waiting for transfers between devices: 264 us -> 0 us
  Pallas kernels: 0 us -> 150 us
  blocking collectives: 72.9 us -> 0 us
  local copies, waits for them, and re-layouts: 72.7 us -> 23.1 us
  other arithmetic: 36.8 us -> 12.2 us
  starting transfers between devices: 21.3 us -> 0 us
  between operations: 14.9 us -> 1.4 us
  matrix products: 38.5 us -> 31.5 us
    psum x4 -> x0, waiting for transfers between devices: 195 us -> none  [the longest x1 76.2 us: on_device(): lax.psum((gain1_g, shift1_g, qkv_g, proj_g, pshift_g, gain2_g, shift2_g,...]
    pallas_call x0 -> x6, Pallas kernels: none -> 150 us  [call(): pl.pallas_call(kernel, out_shape=outs, in_specs=[vmem] * len(args), out_s...]
    all_to_all x3 -> x0, waiting for transfers between devices: 68.6 us -> none  [the longest x2 41.6 us: send_rows(): lax.all_to_all(buffer, 'expert', split_axis=0, concat_axis=0, tiled=True)]
    all_to_all x1 -> x0, blocking collectives: 39.5 us -> none  [return_rows(): lax.all_to_all(ready, 'expert', split_axis=0, concat_axis=0, tiled=True)]
    psum x1 -> x0, blocking collectives: 33.4 us -> none  [on_device(): lax.psum((gain1_g, shift1_g, qkv_g, proj_g, pshift_g, gain2_g, shift2_g,...]
    gather x6 -> x0, local copies, waits for them, and re-layouts: 21.5 us -> none  [the longest x2 6.71 us: on_device(): jnp.take(mixed_b, owners // 2, axis=0, mode='fill', fill_value=0)]
    all_to_all x3 -> x0, starting transfers between devices: 20.9 us -> none  [the longest x2 13.4 us: send_rows(): lax.all_to_all(buffer, 'expert', split_axis=0, concat_axis=0, tiled=True)]
    reduce_sum x10 -> x4, other arithmetic: 19.6 us -> 3.06 us  [the longest x1 1.74 us: fast_device(): pshift_g = jnp.sum(hidden_grad, axis=0)]
  transfers between devices with their start and end apart: 7 -> 0, of which waited for: 7 -> 0; matrix products, arithmetic and copies ran while one was open for 10% -> 0% of each run, Pallas kernels for 0% -> 0%
where the time goes in v1:
time: 219 us; the launch traced here: 218 us
  Pallas kernels  150 us (68%)
  matrix products  31.5 us (14%)
  local copies, waits for them, and re-layouts  23.1 us (11%)
  other arithmetic  12.2 us (6%)
    pallas_call x6, Pallas kernels, call(): pl.pallas_call(kernel, out_shape=outs, in_specs=[vmem] * len(args), out_s...  150 us
    dot_general x6, matrix products, outer_cols(): lax.dot_general(left_b, right_b, (((1,), (1,)), ((), ())), preferred_elem...  9.25 us
    dot_general x5, matrix products, inner_rows(): lax.dot_general(left_b, right_b, (((0,), (0,)), ((), ())), preferred_elem...  7.81 us
    unnamed x63, local copies, waits for them, and re-layouts  6.83 us

profile of v1, /device:TPU:20, one launch (start us, length us, event | category | flops | bytes accessed | tf_op | source)
XLA Modules:
  0.0 218.4 jit_solution(16938468652602612317)
XLA Ops:
  0.8 1.4 convert_reduce_fusion.2
  2.1 1.4 fusion.24
  4.4 1.9 convolution_convert_fusion.5
  6.3 0.7 reshape.268
  7.0 2.5 %fusion.83 = (bf16[2,197,3,1,64]{4,3,2,1,0:T(2,128)(2,1)}, bf16[2,197,3,1,64]{4,3,2,1,0:T(2,128)(2,1)}, bf16[2,197,3,1,64]{4,3,2,1,0:T(2,128)(2,1)}) fusion(bf16[2,197,3,3,64]{4,3,2,1,0:T(4,128)(2,1)S(1)} %reshape.268), kind=kLoop, calls=%fused_computation.162 | loop fusion | bytes 907776 | tf_op jit(solution)/shard_map/slice | solution.py:90
  9.4 1.4 copy.87
  10.8 1.4 copy.86
  12.2 1.0 copy.88
  13.3 1.3 fusion.88
  15.2 0.9 copy.65
  16.1 1.7 reshape.255
  17.8 1.4 convolution_convert_fusion.4.x
  19.3 12.5 %shard_map.263 = bf16[394,768]{1,0:T(8,128)(2,1)S(1)} custom-call(bf16[394,768]{1,0:T(8,128)(2,1)S(1)} %convolution_convert_fusion.4.x), custom_call_target="tpu_custom_call" | custom-call | tf_op jit(solution)/shard_map/pallas_call | solution.py:285
  35.0 25.5 %shard_map.264 = (bf16[8,4,32,768]{3,2,1,0:T(8,128)(2,1)S(1)}, bf16[8,4,32,768]{3,2,1,0:T(8,128)(2,1)S(1)}) custom-call(bf16[8,32,768]{2,1,0:T(8,128)(2,1)S(1)} %bitcast.122, bf16[8,32,768]{2,1,0:T(8,128)(2,1)S(1)} %bitcast.121), custom_call_target="tpu_custom_call" | custom-call | tf_op jit(solution)/shard_map/pallas_call | solution.py:285
  61.4 3.9 %multiply_convert_fusion = (bf16[1024,768]{1,0:T(8,128)(2,1)S(1)}, f32[1024,768]{1,0:T(8,128)S(1)}) fusion(f32[768]{0:T(1024)S(1)} %reduce.1, bf16[1024,768]{1,0:T(8,128)(2,1)S(1)} %bitcast.123, bf16[1,768,768]{2,1,0:T(8,128)(2,1)S(1)} %copy-done), kind=kOutput, calls=%fused_computation.7 | convolution fusion | flops 1212678144 | bytes 7474176 | tf_op jit(solution)/shard_map/dot_general | solution.py:674
  65.3 3.0 %fusion.89 = (f32[768]{0:T(1024)S(1)}, bf16[1024,768]{1,0:T(8,128)(2,1)S(1)}) fusion(f32[1024,768]{1,0:T(8,128)S(1)} %get-tuple-element.70, f32[768]{0:T(1024)S(1)} %reduce.1, bf16[1024,768]{1,0:T(8,128)(2,1)S(1)} %bitcast.117, bf16[1,768,768]{2,1,0:T(8,128)(2,1)S(1)} %copy-done.26), kind=kOutput, calls=%fused_computation.168 | convolution fusion | flops 1217395968 | bytes 7477248 | tf_op jit(solution)/shard_map/dot_general | solution.py:51
  68.9 2.9 %convolution_bitcast_fusion.1 = f32[1,768,768]{2,1,0:T(8,128)} fusion(bf16[1024,768]{1,0:T(8,128)(2,1)S(1)} %bitcast.124, bf16[1024,768]{1,0:T(8,128)(2,1)S(1)} %get-tuple-element.73), kind=kOutput, calls=%fused_computation.19 | convolution fusion | flops 1207959552 | bytes 5505024 | tf_op jit(solution)/shard_map/dot_general | solution.py:45
  71.8 1.4 convolution_convert_fusion
  73.2 2.9 %convolution_bitcast_fusion = f32[1,768,768]{2,1,0:T(8,128)} fusion(bf16[1024,768]{1,0:T(8,128)(2,1)S(1)} %get-tuple-element.69, bf16[1024,768]{1,0:T(8,128)(2,1)S(1)} %bitcast.118), kind=kOutput, calls=%fused_computation.18 | convolution fusion | flops 1207959552 | bytes 5505024 | tf_op jit(solution)/shard_map/dot_general | solution.py:45
  76.0 1.4 convolution_convert_fusion.1
  77.5 33.6 %shard_map.265 = (bf16[8,2,64,384]{3,2,1,0:T(8,128)(2,1)S(1)}, bf16[8,2,64,384]{3,2,1,0:T(8,128)(2,1)S(1)}) custom-call(bf16[8,128,768]{2,1,0:T(8,128)(2,1)S(1)} %bitcast.120, bf16[8,128,768]{2,1,0:T(8,128)(2,1)S(1)} %bitcast.119, f32[1,768]{1,0:T(1,128)S(1)} %copy-done.2), custom_call_target="tpu_custom_call" | custom-call | tf_op jit(solution)/shard_map/pallas_call | solution.py:285
  111.1 0.6 fusion.28.second
  111.8 1.0 select_reduce_fusion.1
  112.8 0.7 convolution_convert_fusion.7.first
  113.6 11.3 %shard_map.266 = (bf16[394,768]{1,0:T(8,128)(2,1)S(1)}, bf16[394,768]{1,0:T(8,128)(2,1)S(1)}, f32[8,512]{1,0:T(8,128)S(1)}) custom-call(bf16[394,384]{1,0:T(8,128)(2,1)S(1)} %convolution_convert_fusion.7.first, bf16[394,384]{1,0:T(8,128)(2,1)S(1)} %fusion.28.second, f32[8,512]{1,0:T(8,128)S(1)} %select_maximum_fusion.gate), custom_call_target="tpu_custom_call" | custom-call | tf_op jit(solution)/shard_map/pallas_call | solution.py:285
  125.1 0.9 multiply_reduce_fusion
  126.1 1.7 fusion.82
  127.8 1.1 convolution_convert_fusion.8
  128.9 1.0 convolution_convert_fusion.13
  130.0 1.1 reshape.264
  131.1 1.0 multiply_reduce_fusion.4
  135.0 1.8 convolution_convert_fusion.3.x
  136.9 12.5 %shard_map.267 = bf16[394,768]{1,0:T(8,128)(2,1)S(1)} custom-call(bf16[394,768]{1,0:T(8,128)(2,1)S(1)} %convolution_convert_fusion.3.x), custom_call_target="tpu_custom_call" | custom-call | tf_op jit(solution)/shard_map/pallas_call | solution.py:285
  149.4 0.7 fusion.27
  150.2 1.5 fusion.23
  152.6 0.8 convolution_convert_fusion.2
  153.6 0.6 copy.74
  154.3 0.8 copy-done.1
  155.1 54.8 %shard_map.268 = (bf16[8,96,768]{2,1,0:T(8,128)(2,1)S(1)}, f32[8,16,128]{2,1,0:T(8,128)S(1)}) custom-call(bf16[8,96,768]{2,1,0:T(8,128)(2,1)S(1)} %bitcast.114, f32[8,16,128]{2,1,0:T(8,128)S(1)} %copy-done.1), custom_call_target="tpu_custom_call" | custom-call | tf_op jit(solution)/shard_map/pallas_call | solution.py:285
  210.0 0.7 slice.88
  210.7 0.7 squeeze.41
  211.4 0.7 squeeze.40
  212.0 0.7 squeeze.39
  212.7 0.7 squeeze.38
  213.4 0.7 squeeze.37
  214.0 0.9 slice.99
  216.2 0.9 convert_bitcast_fusion
  217.1 1.3 convert_element_type.152
  (115 shorter events, 11.6 us)
Async XLA Ops:
  0.6 60.8 %copy-start = (bf16[1,768,768]{2,1,0:T(8,128)(2,1)S(1)}, bf16[1,768,768]{2,1,0:T(8,128)(2,1)}, u32[]{:S(2)}) copy-start(bf16[1,768,768]{2,1,0:T(8,128)(2,1)} %param.25) | copy-start | bytes 3538948
  0.7 3.7 %copy-start.3 = (bf16[394,768]{1,0:T(8,128)(2,1)S(1)}, bf16[394,768]{1,0:T(8,128)(2,1)}, u32[]{:S(2)}) copy-start(bf16[394,768]{1,0:T(8,128)(2,1)} %param.16) | copy-start | bytes 1815556
  0.7 3.7 %copy-start.19 = (f32[768]{0:T(1024)S(1)}, f32[768]{0:T(1024)}, u32[]{:S(2)}) copy-start(f32[768]{0:T(1024)} %param.17) | copy-start | bytes 9220
  0.7 3.0 %copy-start.17 = (s32[394,2]{0,1:T(2,128)S(1)}, s32[394,2]{0,1:T(2,128)}, u32[]{:S(2)}) copy-start(s32[394,2]{0,1:T(2,128)} %param.29) | copy-start | bytes 9460
  0.7 3.7 %copy-start.27 = (f32[768]{0:T(1024)S(1)}, f32[768]{0:T(1024)}, u32[]{:S(2)}) copy-start(f32[768]{0:T(1024)} %param.18) | copy-start | bytes 9220
  0.7 3.0 %copy-start.22 = (s32[394,2]{0,1:T(2,128)S(1)}, s32[394,2]{0,1:T(2,128)}, u32[]{:S(2)}) copy-start(s32[394,2]{0,1:T(2,128)} %param.30) | copy-start | bytes 9460
  0.7 3.0 %copy-start.23 = (f32[1,768]{1,0:T(1,128)S(1)}, f32[1,768]{1,0:T(1,128)}, u32[]{:S(2)}) copy-start(f32[1,768]{1,0:T(1,128)} %param.26) | copy-start | bytes 9220
  9.4 2.8 %copy-start.6 = (bf16[2,197,3,1,64]{4,3,2,1,0:T(2,128)(2,1)S(1)}, bf16[2,197,3,1,64]{4,3,2,1,0:T(2,128)(2,1)}, u32[]{:S(2)}) copy-start(bf16[2,197,3,1,64]{4,3,2,1,0:T(2,128)(2,1)} %get-tuple-element.54) | copy-start | bytes 453892
  10.8 3.8 %copy-start.8 = (bf16[2,197,3,1,64]{1,4,2,0,3:T(8,128)(2,1)}, bf16[2,197,3,1,64]{1,4,2,0,3:T(8,128)(2,1)S(1)}, u32[]{:S(2)}) copy-start(bf16[2,197,3,1,64]{1,4,2,0,3:T(8,128)(2,1)S(1)} %copy.87) | copy-start | bytes 453892
  15.2 17.8 %copy-start.7 = (bf16[2,197,3,64]{1,3,2,0:T(8,128)(2,1)}, bf16[2,197,3,64]{1,3,2,0:T(8,128)(2,1)S(1)}, u32[]{:S(2)}) copy-start(bf16[2,197,3,64]{1,3,2,0:T(8,128)(2,1)S(1)} %fusion.36) | copy-start | bytes 453892
  17.8 14.0 %copy-start.16 = (f32[768]{0:T(1024)S(1)}, f32[768]{0:T(1024)}, u32[]{:S(2)}) copy-start(f32[768]{0:T(1024)} %param.21) | copy-start | bytes 9220
  31.8 0.7 copy-start.18
  31.8 0.7 copy-start.21
  32.5 0.7 copy-start.20
  32.6 1.3 copy-start.15
  61.4 3.9 %copy-start.26 = (bf16[1,768,768]{2,1,0:T(8,128)(2,1)S(1)}, bf16[1,768,768]{2,1,0:T(8,128)(2,1)}, u32[]{:S(2)}) copy-start(bf16[1,768,768]{2,1,0:T(8,128)(2,1)} %param.27) | copy-start | bytes 3538948
  76.0 1.4 copy-start.2
  77.5 33.7 %copy-start.24 = (s32[394,1]{0,1:T(1,128)S(1)}, s32[394,1]{0,1:T(1,128)}, u32[]{:S(2)}) copy-start(s32[394,1]{0,1:T(1,128)} %get-tuple-element.59) | copy-start | bytes 4732
  77.5 33.7 %copy-start.25 = (s32[394,1]{0,1:T(1,128)S(1)}, s32[394,1]{0,1:T(1,128)}, u32[]{:S(2)}) copy-start(s32[394,1]{0,1:T(1,128)} %get-tuple-element.60) | copy-start | bytes 4732
  126.0 1.8 copy-start.11
  127.8 1.1 copy-start.4
  127.8 1.2 copy-start.14
  132.4 0.9 copy-start.9
  132.4 1.2 copy-start.10
  136.9 13.3 %copy-start.5 = (f32[394,768]{1,0:T(8,128)S(1)}, f32[394,768]{1,0:T(8,128)}, u32[]{:S(2)}) copy-start(f32[394,768]{1,0:T(8,128)} %copy-done.4) | copy-start | bytes 3631108
  150.1 2.4 %copy-start.28 = (f32[768]{0:T(1024)S(1)}, f32[768]{0:T(1024)}, u32[]{:S(2)}) copy-start(f32[768]{0:T(1024)} %param.18) | copy-start | bytes 9220
  152.6 1.0 copy-start.13
  154.3 0.8 copy-start.1
  215.0 1.0 copy-start.12

commit v2 on v1

--- a/solution.py
+++ b/solution.py
@@ -276,6 +276,17 @@
     )
 
 
+def turns(count):
+    far = list(range(count // 2, count))
+    near = list(range(1, count // 2))
+    order = []
+    for i, step in enumerate(far):
+        order.append(step)
+        if i < len(near):
+            order.append(near[i])
+    return order
+
+
 def lanes(index, width):
     return pl.ds(pl.multiple_of(index * width, 128), width)
 
@@ -328,7 +339,7 @@
 def dispatch_kernel(first, second, out0, out1, send_far, send_across, send_core, recv, local):
     e, t, a, c, core, across = place()
     count = first.shape[0]
-    peers = [(lax.rem(e + d, count), t) for d in range(1, count)]
+    peers = [(e ^ d, t) for d in range(1, count)]
     greet(peers + [core, across])
     ins, outs = (first, second), (out0, out1)
     sent = []
@@ -342,8 +353,8 @@
         spot = outs[k].at[origin, quarter]
         remote(spot, spot, send_core.at[k, origin, quarter], recv.at[k, origin, quarter], core).wait_recv()
 
-    for d in range(1, count):
-        dst = lax.rem(e + d, count)
+    for d in turns(count):
+        dst = e ^ d
         for k in range(2):
             push(ins[k].at[dst], k, e, t, send_far.at[k, d], (dst, t))
     keeps = []
@@ -354,19 +365,20 @@
         keep.start()
         keeps.append(keep)
     far = 2 * (1 - a) + c
-    for d in range(1, count + 1):
-        if d < count:
-            origin = lax.rem(e - d + count, count)
+    order = turns(count)
+    for i in range(count):
+        if i < count - 1:
+            origin = e ^ order[i]
             for k in range(2):
                 arrive(k, origin, t)
                 push(outs[k].at[origin, t], k, origin, t, send_across.at[k, origin], across)
                 push(outs[k].at[origin, t], k, origin, t, send_core.at[k, origin, t], core)
-        origin = lax.rem(e - d + 1 + count, count)
+        origin = e ^ order[i - 1] if i else e
         for k in range(2):
             arrive(k, origin, far)
             push(outs[k].at[origin, far], k, origin, far, send_core.at[k, origin, far], core)
     for d in range(count):
-        origin = lax.rem(e - d + count, count)
+        origin = e ^ d
         for k in range(2):
             arrive(k, origin, 2 * a + 1 - c)
             arrive(k, origin, 2 * (1 - a) + 1 - c)
@@ -395,14 +407,14 @@
 ):
     e, t, a, c, core, across = place()
     count = part0.shape[0]
-    peers = [(lax.rem(e + d, count), t) for d in range(1, count)]
+    peers = [(e ^ d, t) for d in range(1, count)]
     greet(peers + [core, across])
     parts, outs = (part0, part1), (out0, out1)
     rows = part0.shape[1] // 2
     width = part0.shape[2] // 2
     mine, other = pl.ds(c * rows, rows), pl.ds((1 - c) * rows, rows)
     left, right = lanes(a, width), lanes(1 - a, width)
-    order = [lax.rem(e + d, count) for d in range(1, count + 1)]
+    order = [e ^ d for d in turns(count)] + [e]
     steps = [(dst, k) for dst in order for k in range(2)]
     stage1, stage2, rest = [], [], []
     for dst, k in steps:
@@ -435,8 +447,8 @@
             keep = pltpu.make_async_copy(ready.at[k, dst], outs[k].at[e, c], local.at[k])
             keep.start()
             keeps.append(keep)
-    for d in range(1, count):
-        origin = lax.rem(e - d + count, count)
+    for d in turns(count):
+        origin = e ^ d
         for k in range(2):
             spot = outs[k].at[origin, c]
             remote(spot, spot, send4.at[k, origin], recv3.at[k, origin], core).wait_recv()
@@ -444,7 +456,7 @@
             copy.start()
             rest.append(copy)
     for d in range(count):
-        origin = lax.rem(e - d + count, count)
+        origin = e ^ d
         for k in range(2):
             spot = outs[k].at[origin, 1 - c]
             remote(spot, spot, send4.at[k, origin], recv4.at[k, origin], core).wait_recv()
@@ -516,16 +528,25 @@
     )
 
 
-def expert_sum_kernel(
-    big, small, out, out_small, got1, sgot1, half1, shalf1, got2, sgot2,
-    send1, recv1, send2, recv2, send3, recv3, send4, recv4,
+def final_kernel(
+    big, small, x, out, out_small, out_x, got1, sgot1, half1, shalf1, got2, sgot2,
+    xgot1, xpart, xgot2, tiny, tgot,
+    send1, recv1, send2, recv2, send3, recv3, send4, recv4, xsend, xrecv, tsend, trecv,
 ):
     e, t, a, c, core, across = place()
     z = e // 2
     y = e % 2
     deep = big.shape[0] // 2
     beside = (2 * z + 1 - y, t)
-    greet([beside] + [(2 * lax.rem(z + d, deep) + y, t) for d in range(1, deep)])
+    greet([beside, core, across] + [(2 * lax.rem(z + d, deep) + y, t) for d in range(1, deep)])
+    width = x.shape[1] // 2
+    mine, other = lanes(c, width), lanes(1 - c, width)
+    xcopies = [
+        remote(x.at[:, other], xgot1, xsend.at[0], xrecv.at[0], core),
+        remote(xpart, xgot2, xsend.at[1], xrecv.at[1], across),
+        remote(out_x.at[:, mine], out_x.at[:, mine], xsend.at[2], xrecv.at[2], core),
+    ]
+    xcopies[0].start()
     stage1, stage2, rest = [], [], []
     order = [2, 1, 3, 0]
     for d in order:
@@ -538,6 +559,9 @@
         for copy in pair:
             copy.start()
         stage1.append(pair)
+    xcopies[0].wait()
+    xpart[...] = (x[:, mine].astype(F32) + xgot1[...].astype(F32)).astype(BF16)
+    xcopies[1].start()
     for i, d in enumerate(order):
         zz = lax.rem(z + d, deep)
         chunk = 2 * zz + y
@@ -562,15 +586,30 @@
         total = total + got2[zz].astype(F32)
         stotal = stotal + sgot2[zz]
     out[e] = total.astype(BF16)
-    out_small[e] = stotal
     both = (out, out_small)
-    for d in (2, 1, 3):
-        zz = lax.rem(z + d, deep)
-        for k in range(2):
-            spot = both[k].at[e]
+
+    def spread(k):
+        spot = both[k].at[e]
+        for d in (2, 1, 3):
+            zz = lax.rem(z + d, deep)
             copy = remote(spot, spot, send3.at[k, zz], recv3.at[k, z], (2 * zz + y, t))
             copy.start()
             rest.append(copy)
+
+    spread(0)
+    tiny[0] = stotal
+    copy = remote(tiny.at[0], tgot.at[0], tsend.at[0], trecv.at[0], core)
+    copy.start()
+    copy.wait()
+    tiny[1] = stotal + tgot[0]
+    copy = remote(tiny.at[1], tgot.at[1], tsend.at[1], trecv.at[1], across)
+    copy.start()
+    copy.wait()
+    out_small[e] = tiny[1] + tgot[1]
+    spread(1)
+    xcopies[1].wait()
+    out_x[:, mine] = (xpart[...].astype(F32) + xgot2[...].astype(F32)).astype(BF16)
+    xcopies[2].start()
     for d in (0, 3, 1, 2):
         zz = lax.rem(z + d, deep)
         for k in range(2):
@@ -584,6 +623,7 @@
         for k in range(2):
             spot = both[k].at[2 * zz + 1 - y]
             remote(spot, spot, send4.at[k, zz], recv4.at[k, zz], beside).wait_recv()
+    xcopies[2].wait()
     for pair in stage1:
         for copy in pair:
             copy.wait_send()
@@ -591,18 +631,23 @@
         copy.wait_send()
 
 
-def expert_sum(big, small, number):
+def final_sums(big, small, x, number):
     count, rows, width = big.shape
     deep = count // 2
     dma = pltpu.SemaphoreType.DMA
     large = pltpu.VMEM((deep, rows, width), BF16)
     little = pltpu.VMEM((deep,) + small.shape[1:], F32)
+    half = pltpu.VMEM((x.shape[0], x.shape[1] // 2), BF16)
+    tiny = pltpu.VMEM((2,) + small.shape[1:], F32)
+    shapes = [jax.ShapeDtypeStruct(v.shape, v.dtype) for v in (big, small, x)]
     return call(
-        expert_sum_kernel,
-        (jax.ShapeDtypeStruct(big.shape, BF16), jax.ShapeDtypeStruct(small.shape, F32)),
-        [large, little, large, little, large, little] + [dma((2, deep))] * 8,
+        final_kernel,
+        tuple(shapes),
+        [large, little, large, little, large, little, half, half, half, tiny, tiny]
+        + [dma((2, deep))] * 8
+        + [dma((3,)), dma((3,)), dma((2,)), dma((2,))],
         number,
-        (big, small),
+        (big, small, x),
     )
 
 
@@ -717,23 +762,31 @@
     hidden_gradb = hidden_grad.astype(BF16)
     context_grad = outer_cols(hidden_gradb, proj_weight).astype(BF16)
     qkv_gradb = attend_back(queries, keys_b, values_b, log_total, context_b, context_grad, images)
-    normed_grad = tensor_sum(outer_cols(qkv_gradb, qkv_weight).astype(BF16), 5).astype(F32)
-    gain1_g = jnp.sum(normed_grad * scaled1, axis=0)
-    shift1_g = jnp.sum(normed_grad, axis=0)
-    tokens_grad = hidden_grad + norm_back(normed_grad, scaled1, inverse1, norm1_gain)
+    normed_part = outer_cols(qkv_gradb, qkv_weight)
+    gain1_g = jnp.sum(normed_part * scaled1, axis=0)
+    shift1_g = jnp.sum(normed_part, axis=0)
     qkv_g = inner_rows(normed_b, qkv_gradb)
     proj_g = inner_rows(hidden_gradb, context_b)
     big = jnp.concatenate([qkv_g.astype(BF16), proj_g.astype(BF16)], axis=1)
     wide = big.shape[1]
     small = jnp.concatenate(
-        [jnp.stack([gain1_g, shift1_g, pshift_g, gain2_g, shift2_g]), router_g], axis=0
+        [
+            jnp.stack([gain1_g, shift1_g]),
+            jnp.stack([pshift_g, gain2_g, shift2_g]) / tensor_count,
+            router_g / tensor_count,
+        ],
+        axis=0,
     )
     names = small.shape[0]
     piece = width // experts
     small = jnp.pad(small, ((0, -names % 8), (0, 0)))
     small = small.reshape(small.shape[0], experts, piece).transpose(1, 0, 2)
     small = jnp.pad(small, ((0, 0), (0, 0), (0, -piece % 128)))
-    big, small = expert_sum(big.reshape(experts, piece, wide), small, 6)
+    big, small, normed_sum = final_sums(
+        big.reshape(experts, piece, wide), small, normed_part.astype(BF16), 6
+    )
+    normed_grad = normed_sum.astype(F32)
+    tokens_grad = hidden_grad + norm_back(normed_grad, scaled1, inverse1, norm1_gain)
     big = big.reshape(width, wide)
     small = small[:, :, :piece].transpose(1, 0, 2).reshape(-1, width)
     return (

time: 219 us -> 203 us (0.927)
  Pallas kernels: 150 us -> 129 us
    pallas_call x6 -> x5, Pallas kernels: 150 us -> 129 us  [call(): pl.pallas_call(kernel, out_shape=outs, in_specs=[vmem] * len(args), out_s...]
    unnamed x63 -> x73, local copies, waits for them, and re-layouts: 6.83 us -> 7.89 us
where the time goes in v2:
time: 203 us; the launch traced here: 201 us
  Pallas kernels  129 us (64%)
  matrix products  32.3 us (16%)
  local copies, waits for them, and re-layouts  25.2 us (12%)
  other arithmetic  12.6 us (6%)
    pallas_call x5, Pallas kernels, call(): pl.pallas_call(kernel, out_shape=outs, in_specs=[vmem] * len(args), out_s...  129 us
    dot_general x6, matrix products, outer_cols(): lax.dot_general(left_b, right_b, (((1,), (1,)), ((), ())), preferred_elem...  10.1 us
    unnamed x73, local copies, waits for them, and re-layouts  7.89 us
    dot_general x5, matrix products, inner_rows(): lax.dot_general(left_b, right_b, (((0,), (0,)), ((), ())), preferred_elem...  7.78 us

profile of v2, /device:TPU:20, one launch (start us, length us, event | category | flops | bytes accessed | tf_op | source)
XLA Modules:
  0.0 200.7 jit_solution(2550668790506583796)
XLA Ops:
  0.8 1.4 convert_reduce_fusion.1
  2.1 1.4 fusion.25
  3.6 0.6 add.179
  6.1 1.9 convolution_convert_fusion.4
  8.0 0.7 reshape.268
  8.6 2.5 %fusion.82 = (bf16[2,197,3,1,64]{4,3,2,1,0:T(2,128)(2,1)}, bf16[2,197,3,1,64]{4,3,2,1,0:T(2,128)(2,1)}, bf16[2,197,3,1,64]{4,3,2,1,0:T(2,128)(2,1)}) fusion(bf16[2,197,3,3,64]{4,3,2,1,0:T(4,128)(2,1)S(1)} %reshape.268), kind=kLoop, calls=%fused_computation.164 | loop fusion | bytes 907776 | tf_op jit(solution)/shard_map/slice | solution.py:90
  11.1 1.4 copy.87
  12.5 1.4 copy.86
  13.9 1.0 copy.88
  15.0 1.3 fusion.87
  16.9 0.9 copy.65
  17.8 1.7 reshape.255
  19.5 1.4 convolution_convert_fusion.3.x
  21.0 12.5 %shard_map.263 = bf16[394,768]{1,0:T(8,128)(2,1)S(1)} custom-call(bf16[394,768]{1,0:T(8,128)(2,1)S(1)} %convolution_convert_fusion.3.x), custom_call_target="tpu_custom_call" | custom-call | tf_op jit(solution)/shard_map/pallas_call | solution.py:296
  36.7 28.7 %shard_map.264 = (bf16[8,4,32,768]{3,2,1,0:T(8,128)(2,1)S(1)}, bf16[8,4,32,768]{3,2,1,0:T(8,128)(2,1)S(1)}) custom-call(bf16[8,32,768]{2,1,0:T(8,128)(2,1)S(1)} %bitcast.122, bf16[8,32,768]{2,1,0:T(8,128)(2,1)S(1)} %bitcast.121), custom_call_target="tpu_custom_call" | custom-call | tf_op jit(solution)/shard_map/pallas_call | solution.py:296
  66.4 3.9 %multiply_convert_fusion = (bf16[1024,768]{1,0:T(8,128)(2,1)S(1)}, f32[1024,768]{1,0:T(8,128)S(1)}) fusion(f32[768]{0:T(1024)S(1)} %copy-done.27, bf16[1024,768]{1,0:T(8,128)(2,1)S(1)} %bitcast.123, bf16[1,768,768]{2,1,0:T(8,128)(2,1)S(1)} %copy-done), kind=kOutput, calls=%fused_computation.7 | convolution fusion | flops 1212678144 | bytes 7474176 | tf_op jit(solution)/shard_map/dot_general | solution.py:719
  70.2 3.0 %fusion.88 = (f32[768]{0:T(1024)S(1)}, bf16[1024,768]{1,0:T(8,128)(2,1)S(1)}) fusion(f32[1024,768]{1,0:T(8,128)S(1)} %get-tuple-element.73, f32[768]{0:T(1024)S(1)} %copy-done.27, bf16[1024,768]{1,0:T(8,128)(2,1)S(1)} %bitcast.117, bf16[1,768,768]{2,1,0:T(8,128)(2,1)S(1)} %copy-done.31), kind=kOutput, calls=%fused_computation.170 | convolution fusion | flops 1217395968 | bytes 7477248 | tf_op jit(solution)/shard_map/dot_general | solution.py:51
  73.8 2.9 %convolution_bitcast_fusion.1 = f32[1,768,768]{2,1,0:T(8,128)} fusion(bf16[1024,768]{1,0:T(8,128)(2,1)S(1)} %bitcast.124, bf16[1024,768]{1,0:T(8,128)(2,1)S(1)} %get-tuple-element.77), kind=kOutput, calls=%fused_computation.13 | convolution fusion | flops 1207959552 | bytes 5505024 | tf_op jit(solution)/shard_map/dot_general | solution.py:45
  76.7 1.4 convolution_convert_fusion
  78.1 2.9 %convolution_bitcast_fusion = f32[1,768,768]{2,1,0:T(8,128)} fusion(bf16[1024,768]{1,0:T(8,128)(2,1)S(1)} %get-tuple-element.72, bf16[1024,768]{1,0:T(8,128)(2,1)S(1)} %bitcast.118), kind=kOutput, calls=%fused_computation.12 | convolution fusion | flops 1207959552 | bytes 5505024 | tf_op jit(solution)/shard_map/dot_general | solution.py:45
  81.0 1.4 convolution_convert_fusion.1
  82.4 29.9 %shard_map.265 = (bf16[8,2,64,384]{3,2,1,0:T(8,128)(2,1)S(1)}, bf16[8,2,64,384]{3,2,1,0:T(8,128)(2,1)S(1)}) custom-call(bf16[8,128,768]{2,1,0:T(8,128)(2,1)S(1)} %bitcast.120, bf16[8,128,768]{2,1,0:T(8,128)(2,1)S(1)} %bitcast.119, f32[1,768]{1,0:T(1,128)S(1)} %copy-done.3), custom_call_target="tpu_custom_call" | custom-call | tf_op jit(solution)/shard_map/pallas_call | solution.py:296
  112.3 0.6 fusion.28.second
  113.0 1.0 select_reduce_fusion.1
  114.0 0.7 convolution_convert_fusion.6.first
  114.7 11.3 %shard_map.266 = (bf16[394,768]{1,0:T(8,128)(2,1)S(1)}, bf16[394,768]{1,0:T(8,128)(2,1)S(1)}, f32[8,512]{1,0:T(8,128)S(1)}) custom-call(bf16[394,384]{1,0:T(8,128)(2,1)S(1)} %convolution_convert_fusion.6.first, bf16[394,384]{1,0:T(8,128)(2,1)S(1)} %fusion.28.second, f32[8,512]{1,0:T(8,128)S(1)} %select_maximum_fusion.3.gate), custom_call_target="tpu_custom_call" | custom-call | tf_op jit(solution)/shard_map/pallas_call | solution.py:296
  126.2 0.9 multiply_reduce_fusion
  127.2 1.7 fusion.81
  129.0 1.1 convolution_convert_fusion.7
  130.1 1.0 convolution_convert_fusion.12
  131.1 1.1 reshape.264
  132.2 1.0 multiply_reduce_fusion.4
  136.2 2.7 %fusion.20 = (f32[768]{0:T(1024)S(1)}, f32[768]{0:T(1024)S(1)}, bf16[394,768]{1,0:T(8,128)(2,1)}) fusion(bf16[394,768]{1,0:T(8,128)(2,1)S(1)} %copy-done.4, f32[394]{0:T(512)S(1)} %add_rsqrt_fusion.1, f32[394]{0:T(512)S(1)} %broadcast_multiply_fusion.5, bf16[394,576]{0,1:T(8,128)(2,1)S(1)} %convert_element_type.147, bf16[768,576]{0,1:T(8,128)(2,1)} %param.19), kind=kOutput, calls=%fused_computation.43 | convolution fusion | flops 350702592 | bytes 2558288 | tf_op jit(solution)/shard_map/dot_general | solution.py:51
  139.7 0.8 convolution_convert_fusion.2
  140.7 0.6 copy.74
  141.4 1.1 copy-done.1
  142.5 0.8 copy-done.2
  143.3 46.9 %shard_map.267 = (bf16[8,96,768]{2,1,0:T(8,128)(2,1)S(1)}, f32[8,16,128]{2,1,0:T(8,128)S(1)}, bf16[394,768]{1,0:T(8,128)(2,1)S(1)}) custom-call(bf16[8,96,768]{2,1,0:T(8,128)(2,1)S(1)} %bitcast.114, f32[8,16,128]{2,1,0:T(8,128)S(1)} %copy-done.2, bf16[394,768]{1,0:T(8,128)(2,1)S(1)} %copy-done.1), custom_call_target="tpu_custom_call" | custom-call | tf_op jit(solution)/shard_map/pallas_call | solution.py:296
  190.7 1.5 fusion.24
  192.3 0.7 slice.88
  193.0 0.7 squeeze.41
  193.7 0.7 squeeze.40
  194.4 0.7 squeeze.39
  195.0 0.7 squeeze.38
  195.7 0.7 squeeze.37
  196.4 0.9 slice.99
  198.5 0.9 convert_bitcast_fusion
  199.4 1.3 convert_element_type.152
  (124 shorter events, 13.0 us)
Async XLA Ops:
  0.6 65.7 %copy-start = (bf16[1,768,768]{2,1,0:T(8,128)(2,1)S(1)}, bf16[1,768,768]{2,1,0:T(8,128)(2,1)}, u32[]{:S(2)}) copy-start(bf16[1,768,768]{2,1,0:T(8,128)(2,1)} %param.25) | copy-start | bytes 3538948
  0.7 5.4 %copy-start.4 = (bf16[394,768]{1,0:T(8,128)(2,1)S(1)}, bf16[394,768]{1,0:T(8,128)(2,1)}, u32[]{:S(2)}) copy-start(bf16[394,768]{1,0:T(8,128)(2,1)} %param.16) | copy-start | bytes 1815556
  0.7 5.4 %copy-start.21 = (f32[768]{0:T(1024)S(1)}, f32[768]{0:T(1024)}, u32[]{:S(2)}) copy-start(f32[768]{0:T(1024)} %param.17) | copy-start | bytes 9220
  0.7 4.2 %copy-start.19 = (s32[394,2]{0,1:T(2,128)S(1)}, s32[394,2]{0,1:T(2,128)}, u32[]{:S(2)}) copy-start(s32[394,2]{0,1:T(2,128)} %param.29) | copy-start | bytes 9460
  0.7 5.4 %copy-start.32 = (f32[768]{0:T(1024)S(1)}, f32[768]{0:T(1024)}, u32[]{:S(2)}) copy-start(f32[768]{0:T(1024)} %param.18) | copy-start | bytes 9220
  0.7 4.1 %copy-start.25 = (s32[394,2]{0,1:T(2,128)S(1)}, s32[394,2]{0,1:T(2,128)}, u32[]{:S(2)}) copy-start(s32[394,2]{0,1:T(2,128)} %param.30) | copy-start | bytes 9460
  0.7 3.5 %copy-start.28 = (f32[1,768]{1,0:T(1,128)S(1)}, f32[1,768]{1,0:T(1,128)}, u32[]{:S(2)}) copy-start(f32[1,768]{1,0:T(1,128)} %param.26) | copy-start | bytes 9220
  11.1 2.8 %copy-start.8 = (bf16[2,197,3,1,64]{4,3,2,1,0:T(2,128)(2,1)S(1)}, bf16[2,197,3,1,64]{4,3,2,1,0:T(2,128)(2,1)}, u32[]{:S(2)}) copy-start(bf16[2,197,3,1,64]{4,3,2,1,0:T(2,128)(2,1)} %get-tuple-element.57) | copy-start | bytes 453892
  12.5 3.8 %copy-start.10 = (bf16[2,197,3,1,64]{1,4,2,0,3:T(8,128)(2,1)}, bf16[2,197,3,1,64]{1,4,2,0,3:T(8,128)(2,1)S(1)}, u32[]{:S(2)}) copy-start(bf16[2,197,3,1,64]{1,4,2,0,3:T(8,128)(2,1)S(1)} %copy.87) | copy-start | bytes 453892
  16.9 17.8 %copy-start.9 = (bf16[2,197,3,64]{1,3,2,0:T(8,128)(2,1)}, bf16[2,197,3,64]{1,3,2,0:T(8,128)(2,1)S(1)}, u32[]{:S(2)}) copy-start(bf16[2,197,3,64]{1,3,2,0:T(8,128)(2,1)S(1)} %fusion.36) | copy-start | bytes 453892
  19.5 14.0 %copy-start.18 = (f32[768]{0:T(1024)S(1)}, f32[768]{0:T(1024)}, u32[]{:S(2)}) copy-start(f32[768]{0:T(1024)} %param.21) | copy-start | bytes 9220
  33.5 0.7 copy-start.20
  33.5 0.7 copy-start.24
  34.2 0.7 copy-start.22
  34.3 1.0 copy-start.23
  34.3 1.0 copy-start.26
  34.3 1.3 copy-start.17
  36.7 29.7 %copy-start.27 = (f32[768]{0:T(1024)S(1)}, f32[768]{0:T(1024)}, u32[]{:S(2)}) copy-start(f32[768]{0:T(1024)} %reduce.1) | copy-start | bytes 9220
  66.4 3.9 %copy-start.31 = (bf16[1,768,768]{2,1,0:T(8,128)(2,1)S(1)}, bf16[1,768,768]{2,1,0:T(8,128)(2,1)}, u32[]{:S(2)}) copy-start(bf16[1,768,768]{2,1,0:T(8,128)(2,1)} %param.27) | copy-start | bytes 3538948
  81.0 1.4 copy-start.3
  82.4 29.9 %copy-start.29 = (s32[394,1]{0,1:T(1,128)S(1)}, s32[394,1]{0,1:T(1,128)}, u32[]{:S(2)}) copy-start(s32[394,1]{0,1:T(1,128)} %get-tuple-element.62) | copy-start | bytes 4732
  82.4 29.9 %copy-start.30 = (s32[394,1]{0,1:T(1,128)S(1)}, s32[394,1]{0,1:T(1,128)}, u32[]{:S(2)}) copy-start(s32[394,1]{0,1:T(1,128)} %get-tuple-element.63) | copy-start | bytes 4732
  127.2 1.8 copy-start.13
  128.9 1.1 copy-start.6
  128.9 1.2 copy-start.16
  133.6 0.9 copy-start.11
  133.6 1.2 copy-start.12
  136.1 3.5 %copy-start.33 = (f32[768]{0:T(1024)S(1)}, f32[768]{0:T(1024)}, u32[]{:S(2)}) copy-start(f32[768]{0:T(1024)} %param.18) | copy-start | bytes 9220
  139.7 1.0 copy-start.15
  141.4 1.1 copy-start.1
  142.4 0.8 copy-start.2
  143.3 46.9 %copy-start.5 = (bf16[394,768]{1,0:T(8,128)(2,1)S(1)}, bf16[394,768]{1,0:T(8,128)(2,1)}, u32[]{:S(2)}) copy-start(bf16[394,768]{1,0:T(8,128)(2,1)} %param.16) | copy-start | bytes 1815556
  143.3 47.4 %copy-start.7 = (f32[394,768]{1,0:T(8,128)S(1)}, f32[394,768]{1,0:T(8,128)}, u32[]{:S(2)}) copy-start(f32[394,768]{1,0:T(8,128)} %copy-done.6) | copy-start | bytes 3631108
  197.4 1.0 copy-start.14

commit v3 on v2

--- a/solution.py
+++ b/solution.py
@@ -336,148 +336,184 @@
     )
 
 
-def dispatch_kernel(first, second, out0, out1, send_far, send_across, send_core, recv, local):
-    e, t, a, c, core, across = place()
-    count = first.shape[0]
-    peers = [(e ^ d, t) for d in range(1, count)]
-    greet(peers + [core, across])
-    ins, outs = (first, second), (out0, out1)
-    sent = []
-
-    def push(src, k, origin, quarter, send, device):
-        copy = remote(src, outs[k].at[origin, quarter], send, recv.at[k, origin, quarter], device)
-        copy.start()
-        sent.append(copy)
-
-    def arrive(k, origin, quarter):
-        spot = outs[k].at[origin, quarter]
-        remote(spot, spot, send_core.at[k, origin, quarter], recv.at[k, origin, quarter], core).wait_recv()
-
-    for d in turns(count):
-        dst = e ^ d
-        for k in range(2):
-            push(ins[k].at[dst], k, e, t, send_far.at[k, d], (dst, t))
-    keeps = []
-    for k in range(2):
-        push(ins[k].at[e], k, e, t, send_across.at[k, e], across)
-        push(ins[k].at[e], k, e, t, send_core.at[k, e, t], core)
-        keep = pltpu.make_async_copy(ins[k].at[e], outs[k].at[e, t], local.at[k])
-        keep.start()
-        keeps.append(keep)
-    far = 2 * (1 - a) + c
-    order = turns(count)
-    for i in range(count):
-        if i < count - 1:
-            origin = e ^ order[i]
-            for k in range(2):
-                arrive(k, origin, t)
-                push(outs[k].at[origin, t], k, origin, t, send_across.at[k, origin], across)
-                push(outs[k].at[origin, t], k, origin, t, send_core.at[k, origin, t], core)
-        origin = e ^ order[i - 1] if i else e
-        for k in range(2):
-            arrive(k, origin, far)
-            push(outs[k].at[origin, far], k, origin, far, send_core.at[k, origin, far], core)
-    for d in range(count):
-        origin = e ^ d
-        for k in range(2):
-            arrive(k, origin, 2 * a + 1 - c)
-            arrive(k, origin, 2 * (1 - a) + 1 - c)
-    for copy in sent:
-        copy.wait_send()
-    for keep in keeps:
-        keep.wait()
-
-
-def dispatch(first, second, number):
-    count, rows, width = first.shape
-    out = jax.ShapeDtypeStruct((count, 4, rows, width), BF16)
-    dma = pltpu.SemaphoreType.DMA
-    return call(
-        dispatch_kernel,
-        (out, out),
-        [dma((2, count)), dma((2, count)), dma((2, count, 4)), dma((2, count, 4)), dma((2,))],
-        number,
-        (first, second),
-    )
-
-
-def collect_kernel(
-    part0, part1, shift, out0, out1, got1, half1, got2, ready,
+def expert_kernel(
+    first, second, up_w, up_b, down_w, shift,
+    rows_in, grads_in, activ, pre_b, bias_grad, out0, out1,
+    part, got1, half1, got2, ready,
+    send_far, send_across, send_core, recv,
     send1, recv1, send2, recv2, send3, recv3, send4, recv4, local,
 ):
     e, t, a, c, core, across = place()
-    count = part0.shape[0]
-    peers = [(e ^ d, t) for d in range(1, count)]
-    greet(peers + [core, across])
-    parts, outs = (part0, part1), (out0, out1)
-    rows = part0.shape[1] // 2
-    width = part0.shape[2] // 2
+    count = first.shape[0]
+    greet([(e ^ d, t) for d in range(1, count)] + [core, across])
+    ins, taken, outs = (first, second), (rows_in, grads_in), (out0, out1)
+    far = 2 * (1 - a) + c
+    near, cross = 2 * a + 1 - c, 2 * (1 - a) + 1 - c
+    rows, width = part.shape[2] // 2, part.shape[3] // 2
     mine, other = pl.ds(c * rows, rows), pl.ds((1 - c) * rows, rows)
     left, right = lanes(a, width), lanes(1 - a, width)
-    order = [e ^ d for d in turns(count)] + [e]
-    steps = [(dst, k) for dst in order for k in range(2)]
-    stage1, stage2, rest = [], [], []
-    for dst, k in steps:
-        copy = remote(parts[k].at[dst, other], got1.at[k, dst], send1.at[k, dst], recv1.at[k, dst], core)
-        copy.start()
-        stage1.append(copy)
-    for i, (dst, k) in enumerate(steps):
-        stage1[i].wait_recv()
-        half1[k, dst] = (parts[k][dst, mine].astype(F32) + got1[k, dst].astype(F32)).astype(BF16)
-        copy = remote(
+
+    def origin_of(i):
+        return e ^ (i // 2 + (i % 2) * (count // 2))
+
+    def far_copy(k, dst):
+        return remote(ins[k].at[dst], taken[k].at[e, t], send_far.at[k, dst], recv.at[k, e, t], (dst, t))
+
+    def across_copy(k, origin):
+        spot = taken[k].at[origin, t]
+        return remote(spot, spot, send_across.at[k, origin], recv.at[k, origin, t], across)
+
+    def core_copy(k, origin, quarter):
+        spot = taken[k].at[origin, quarter]
+        return remote(spot, spot, send_core.at[k, origin, quarter], recv.at[k, origin, quarter], core)
+
+    def one_copy(k, dst):
+        return remote(part.at[k, dst, other], got1.at[k, dst], send1.at[k, dst], recv1.at[k, dst], core)
+
+    def two_copy(k, dst):
+        return remote(
             half1.at[k, dst, :, right], got2.at[k, dst], send2.at[k, dst], recv2.at[k, dst], across
         )
-        copy.start()
-        stage2.append(copy)
-    keeps = []
-    for i, (dst, k) in enumerate(steps):
-        stage2[i].wait_recv()
-        total = half1[k, dst, :, left].astype(F32) + got2[k, dst].astype(F32)
-        if k == 0:
-            total = total + shift[:, left]
-        ready[k, dst] = total.astype(BF16)
-        if i < len(steps) - 2:
-            copy = remote(ready.at[k, dst], outs[k].at[e, c], send3.at[k, dst], recv3.at[k, e], (dst, t))
-            copy.start()
-            rest.append(copy)
-        else:
-            copy = remote(ready.at[k, dst], outs[k].at[e, c], send4.at[k, e], recv4.at[k, e], core)
-            copy.start()
-            rest.append(copy)
-            keep = pltpu.make_async_copy(ready.at[k, dst], outs[k].at[e, c], local.at[k])
-            keep.start()
-            keeps.append(keep)
+
+    def three_copy(k, dst):
+        return remote(ready.at[k, dst], outs[k].at[e, c], send3.at[k, dst], recv3.at[k, e], (dst, t))
+
+    def four_copy(k, origin, side):
+        spot = outs[k].at[origin, side]
+        return remote(spot, spot, send4.at[k, origin], recv4.at[k, origin], core)
+
+    for d in turns(count):
+        for k in range(2):
+            far_copy(k, e ^ d).start()
+    keeps = [pltpu.make_async_copy(ins[k].at[e], taken[k].at[e, t], local.at[k]) for k in range(2)]
+    for keep in keeps:
+        keep.start()
+    bias_grad[...] = jnp.zeros_like(bias_grad)
+    for keep in keeps:
+        keep.wait()
+
+    def step(i, carry):
+        @pl.when(i < count)
+        def _():
+            origin = origin_of(i)
+            for k in range(2):
+
+                @pl.when(i > 0)
+                def _():
+                    core_copy(k, origin, t).wait_recv()
+
+                across_copy(k, origin).start()
+                core_copy(k, origin, t).start()
+
+        @pl.when((i >= 1) & (i < count + 1))
+        def _():
+            origin = origin_of(i - 1)
+            for k in range(2):
+                core_copy(k, origin, far).wait_recv()
+                core_copy(k, origin, far).start()
+
+        @pl.when((i >= 2) & (i < count + 2))
+        def _():
+            origin = origin_of(i - 2)
+            for k in range(2):
+                core_copy(k, origin, near).wait_recv()
+                core_copy(k, origin, cross).wait_recv()
+            tokens = rows_in[origin].reshape(2 * rows, 2 * width)
+            grads = grads_in[origin].reshape(2 * rows, 2 * width)
+            preact = jnp.dot(tokens, up_w[...], preferred_element_type=F32) + up_b[...]
+            bell = 0.5 * (1.0 + lax.erf(preact * half_root))
+            active = (preact * bell).astype(BF16)
+            activ[origin] = active
+            part[0, origin] = jnp.dot(active, down_w[...], preferred_element_type=F32).astype(BF16)
+            one_copy(0, origin).start()
+            slope = bell + preact * jnp.exp(-0.5 * preact * preact) * gauss_peak
+            pre_grad = outer_cols(grads, down_w[...]) * slope
+            bias_grad[...] += jnp.sum(pre_grad, axis=0, keepdims=True)
+            pre_low = pre_grad.astype(BF16)
+            pre_b[origin] = pre_low
+            part[1, origin] = outer_cols(pre_low, up_w[...]).astype(BF16)
+            one_copy(1, origin).start()
+
+        @pl.when((i >= 3) & (i < count + 3))
+        def _():
+            dst = origin_of(i - 3)
+            for k in range(2):
+                one_copy(k, dst).wait_recv()
+                half1[k, dst] = (
+                    part[k, dst, mine].astype(F32) + got1[k, dst].astype(F32)
+                ).astype(BF16)
+                two_copy(k, dst).start()
+
+        @pl.when(i >= 4)
+        def _():
+            dst = origin_of(i - 4)
+            for k in range(2):
+                two_copy(k, dst).wait_recv()
+                total = half1[k, dst, :, left].astype(F32) + got2[k, dst].astype(F32)
+                if k == 0:
+                    total = total + shift[:, left]
+                ready[k, dst] = total.astype(BF16)
+
+                @pl.when(i == 4)
+                def _():
+                    keep = pltpu.make_async_copy(ready.at[k, dst], outs[k].at[e, c], local.at[k])
+                    keep.start()
+                    keep.wait()
+                    four_copy(k, e, c).start()
+
+                @pl.when(i > 4)
+                def _():
+                    three_copy(k, dst).start()
+
+        return carry
+
+    lax.fori_loop(0, count + 4, step, 0)
     for d in turns(count):
         origin = e ^ d
         for k in range(2):
             spot = outs[k].at[origin, c]
             remote(spot, spot, send4.at[k, origin], recv3.at[k, origin], core).wait_recv()
-            copy = remote(spot, spot, send4.at[k, origin], recv4.at[k, origin], core)
-            copy.start()
-            rest.append(copy)
-    for d in range(count):
+            four_copy(k, origin, c).start()
+
+    def finish(d, carry):
         origin = e ^ d
         for k in range(2):
-            spot = outs[k].at[origin, 1 - c]
-            remote(spot, spot, send4.at[k, origin], recv4.at[k, origin], core).wait_recv()
-    for copy in stage1 + stage2 + rest:
-        copy.wait_send()
-    for keep in keeps:
-        keep.wait()
-
-
-def collect(part0, part1, shift, number):
-    count, rows, width = part0.shape
-    out = jax.ShapeDtypeStruct((count, 2, rows // 2, width // 2), BF16)
+            four_copy(k, origin, 1 - c).wait_recv()
+            across_copy(k, origin).wait_send()
+            core_copy(k, origin, t).wait_send()
+            core_copy(k, origin, far).wait_send()
+            one_copy(k, origin).wait_send()
+            two_copy(k, origin).wait_send()
+            four_copy(k, origin, c).wait_send()
+
+            @pl.when(d > 0)
+            def _():
+                far_copy(k, origin).wait_send()
+                three_copy(k, origin).wait_send()
+
+        return carry
+
+    lax.fori_loop(0, count, finish, 0)
+
+
+def run_experts(first, second, up_w, up_b, down_w, shift, number):
+    count, rows, width = first.shape
+    hidden = up_w.shape[1]
+    taken = jax.ShapeDtypeStruct((count, 4, rows, width), BF16)
+    inner = jax.ShapeDtypeStruct((count, 4 * rows, hidden), BF16)
+    out = jax.ShapeDtypeStruct((count, 2, 2 * rows, width // 2), BF16)
     dma = pltpu.SemaphoreType.DMA
-    full = pltpu.VMEM((2, count, rows // 2, width), BF16)
-    half = pltpu.VMEM((2, count, rows // 2, width // 2), BF16)
+    full = pltpu.VMEM((2, count, 2 * rows, width), BF16)
+    half = pltpu.VMEM((2, count, 2 * rows, width // 2), BF16)
     return call(
-        collect_kernel,
-        (out, out),
-        [full, full, half, half] + [dma((2, count))] * 8 + [dma((2,))],
+        expert_kernel,
+        (taken, taken, inner, inner, jax.ShapeDtypeStruct((1, hidden), F32), out, out),
+        [pltpu.VMEM((2, count, 4 * rows, width), BF16), full, full, half, half]
+        + [dma((2, count)), dma((2, count)), dma((2, count, 4)), dma((2, count, 4))]
+        + [dma((2, count))] * 8
+        + [dma((2,))],
         number,
-        (part0, part1, shift),
+        (first, second, up_w, up_b, down_w, shift),
     )
 
 
@@ -711,29 +747,24 @@
     )
     rows_out = jnp.dot(chooser, mixed_b, preferred_element_type=F32).astype(BF16)
     grad_out = (slot_gate * jnp.dot(chooser, cotangent, preferred_element_type=F32)).astype(BF16)
-    received, grad_recv = dispatch(
-        rows_out.reshape(experts, quarter, width), grad_out.reshape(experts, quarter, width), 2
+    received, grad_recv, activ_b, pre_gradb, eshift_g, returned, back_rows = run_experts(
+        rows_out.reshape(experts, quarter, width),
+        grad_out.reshape(experts, quarter, width),
+        expand_weight[0],
+        expand_shift,
+        shrink_weight[0],
+        shrink_shift,
+        2,
     )
     received = received.reshape(experts * padded, width)
     grad_recv = grad_recv.reshape(experts * padded, width)
-    preact = jnp.dot(received, expand_weight[0], preferred_element_type=F32) + expand_shift[0]
-    activ_b = gelu_exact(preact).astype(BF16)
-    out_part = jnp.dot(activ_b, shrink_weight[0], preferred_element_type=F32).astype(BF16)
-    pre_grad = outer_cols(grad_recv, shrink_weight[0]) * gelu_slope(preact)
-    pre_gradb = pre_grad.astype(BF16)
-    rows_part = outer_cols(pre_gradb, expand_weight[0]).astype(BF16)
-    returned, back_rows = collect(
-        out_part.reshape(experts, padded, width),
-        rows_part.reshape(experts, padded, width),
-        shrink_shift,
-        3,
-    )
+    activ_b = activ_b.reshape(experts * padded, -1)
+    pre_gradb = pre_gradb.reshape(experts * padded, -1)
     returned = returned.reshape(experts * padded, half)
     back_rows = back_rows.reshape(experts * padded, half)
     shrink_g = inner_rows(activ_b, grad_recv)
     sshift_g = jnp.sum(grad_recv.astype(F32), axis=0)
     expand_g = inner_rows(received, pre_gradb)
-    eshift_g = jnp.sum(pre_grad, axis=0)
     upstream = cotangent.astype(F32)
     slots = lax.broadcasted_iota(jnp.int32, (tok_count, experts * padded), 1)
     marks = [slots == spots[:, j : j + 1] for j in range(2)]
@@ -801,7 +832,7 @@
         small[4],
         small[5:names].T,
         expand_g[None],
-        eshift_g[None],
+        eshift_g,
         shrink_g[None],
         sshift_g[None],
     )

time: 203 us -> 185 us (0.911)
  the two profiles are of different devices: /device:TPU:20 before, /device:TPU:8 now
where the time goes in v3:
time: 185 us; the launch traced here: 184 us
  Pallas kernels  131 us (71%)
  local copies, waits for them, and re-layouts  20.4 us (11%)
  matrix products  20.1 us (11%)
  other arithmetic  11.1 us (6%)
    pallas_call x4, Pallas kernels, call(): pl.pallas_call(kernel, out_shape=outs, in_specs=[vmem] * len(args), out_s...  131 us
    unnamed x78, local copies, waits for them, and re-layouts  9.19 us
    dot_general x5, matrix products, inner_rows(): lax.dot_general(left_b, right_b, (((0,), (0,)), ((), ())), preferred_elem...  8.88 us
    dot_general x4, matrix products, outer_cols(): lax.dot_general(left_b, right_b, (((1,), (1,)), ((), ())), preferred_elem...  3.86 us

profile of v3, /device:TPU:8, one launch (start us, length us, event | category | flops | bytes accessed | tf_op | source)
XLA Modules:
  0.0 184.4 jit_solution(13275633554773391728)
XLA Ops:
  0.7 1.3 convert_reduce_fusion.1
  2.1 1.4 fusion.20
  3.7 0.8 convolution_convert_fusion.2
  4.5 0.7 reshape.268
  5.2 2.3 %fusion.70 = (bf16[2,197,3,1,64]{4,3,2,1,0:T(2,128)(2,1)}, bf16[2,197,3,1,64]{4,3,2,1,0:T(2,128)(2,1)}, bf16[2,197,3,1,64]{4,3,2,1,0:T(2,128)(2,1)S(1)}) fusion(bf16[2,197,3,3,64]{4,3,2,1,0:T(4,128)(2,1)S(1)} %reshape.268), kind=kLoop, calls=%fused_computation.147 | loop fusion | bytes 907776 | tf_op jit(solution)/shard_map/slice | solution.py:90
  7.5 1.3 copy.87
  8.8 1.3 copy.86
  10.1 0.4 copy.88
  10.6 0.4 fusion.75
  11.3 0.8 copy-done.8
  13.1 12.5 %shard_map.263 = bf16[394,768]{1,0:T(8,128)(2,1)S(1)} custom-call(bf16[394,768]{1,0:T(8,128)(2,1)S(1)} %convolution_convert_fusion.1.x), custom_call_target="tpu_custom_call" | custom-call | tf_op jit(solution)/shard_map/pallas_call | solution.py:296
  26.0 0.4 multiply_reduce_fusion.2
  27.8 0.6 fusion.12
  28.3 0.6 convolution_convert_fusion.3
  29.4 57.3 %shard_map.264 = (bf16[8,4,32,768]{3,2,1,0:T(8,128)(2,1)}, bf16[8,4,32,768]{3,2,1,0:T(8,128)(2,1)}, bf16[8,128,768]{2,1,0:T(8,128)(2,1)}, bf16[8,128,768]{2,1,0:...) custom-call(bf16[8,32,768]{2,1,0:T(8,128)(2,1)S(1)} %bitcast.104, ...), custom_call_target="tpu_custom_call" | custom-call | tf_op jit(solution)/shard_map/pallas_call | solution.py:296
  86.6 0.6 fusion.23.second
  87.3 1.0 select_reduce_fusion.1
  88.3 0.7 convolution_convert_fusion.4.first
  89.0 0.7 copy-done.16
  90.0 0.6 broadcast_in_dim.106
  90.6 11.2 %shard_map.265 = (bf16[394,768]{1,0:T(8,128)(2,1)S(1)}, bf16[394,768]{1,0:T(8,128)(2,1)S(1)}, f32[8,512]{1,0:T(8,128)S(1)}) custom-call(bf16[394,384]{1,0:T(8,128)(2,1)S(1)} %convolution_convert_fusion.4.first, bf16[394,384]{1,0:T(8,128)(2,1)S(1)} %fusion.23.second, f32[8,512]{1,0:T(8,128)S(1)} %select_maximum_fusion.3.gate), custom_call_target="tpu_custom_call" | custom-call | tf_op jit(solution)/shard_map/pallas_call | solution.py:296
  102.0 0.9 multiply_reduce_fusion
  103.0 1.7 fusion.69
  104.8 1.1 convolution_convert_fusion.5
  106.5 1.7 fusion.29
  108.3 0.4 fusion.11
  109.6 0.6 copy.73
  110.5 1.6 fusion.15
  112.3 1.9 %convolution_convert_fusion = bf16[768,576]{0,1:T(8,128)(2,1)S(1)} fusion(bf16[394,576]{0,1:T(8,128)(2,1)} %copy-done.23, bf16[394,768]{1,0:T(8,128)(2,1)S(1)} %copy-done.6, f32[768]{0:T(1024)S(1)} %copy-done.35, f32[768]{0:T(1024)S(1)} %copy-done.27, f32[394]{0:T(512)S(1)} %add_rsqrt_fusion.1, f32[394]{0:T(512)S(1)} %broadcast_multiply_fusion.5), kind=kOutput, calls=%fused_computation.19 | convolution fusion | flops 350843904 | bytes 1953104 | tf_op jit(solution)/shard_map/dot_general | solution.py:45
  114.3 0.9 copy.74
  115.3 1.1 copy-done.3
  116.3 50.4 %shard_map.266 = (bf16[8,96,768]{2,1,0:T(8,128)(2,1)S(1)}, f32[8,16,128]{2,1,0:T(8,128)S(1)}, bf16[394,768]{1,0:T(8,128)(2,1)S(1)}) custom-call(bf16[8,96,768]{2,1,0:T(8,128)(2,1)S(1)} %bitcast.98, f32[8,16,128]{2,1,0:T(8,128)S(1)} %pad.14.small, bf16[394,768]{1,0:T(8,128)(2,1)S(1)} %copy-done.3), custom_call_target="tpu_custom_call" | custom-call | tf_op jit(solution)/shard_map/pallas_call | solution.py:296
  166.8 0.5 fusion.22
  167.3 1.5 fusion.19
  168.9 0.7 slice.88
  169.6 0.7 squeeze.39
  170.3 0.7 squeeze.38
  170.9 0.7 squeeze.37
  171.6 0.7 squeeze.36
  172.3 0.7 squeeze.35
  172.9 0.9 slice.99
  174.0 0.6 copy.89
  175.1 0.9 convert_bitcast_fusion
  176.0 1.3 convert_element_type.136
  177.3 0.8 copy-done.32
  178.1 2.8 %convolution_bitcast_fusion.1 = f32[1,768,768]{2,1,0:T(8,128)} fusion(bf16[1024,768]{1,0:T(8,128)(2,1)S(1)} %bitcast.136, bf16[1024,768]{1,0:T(8,128)(2,1)S(1)} %bitcast.137), kind=kOutput, calls=%fused_computation.5 | convolution fusion | flops 1207959552 | bytes 5505024 | tf_op jit(solution)/shard_map/dot_general | solution.py:45
  181.0 2.8 %convolution_bitcast_fusion = f32[1,768,768]{2,1,0:T(8,128)} fusion(bf16[1024,768]{1,0:T(8,128)(2,1)S(1)} %bitcast.135, bf16[1024,768]{1,0:T(8,128)(2,1)S(1)} %bitcast.108), kind=kOutput, calls=%fused_computation.4 | convolution fusion | flops 1207959552 | bytes 5505024 | tf_op jit(solution)/shard_map/dot_general | solution.py:45
  183.8 0.6 copy.99
  (122 shorter events, 7.0 us)
Async XLA Ops:
  0.6 3.1 %copy-start = (bf16[768,576]{0,1:T(8,128)(2,1)S(1)}, bf16[768,576]{0,1:T(8,128)(2,1)}, u32[]{:S(2)}) copy-start(bf16[768,576]{0,1:T(8,128)(2,1)} %param.19) | copy-start | bytes 2654212
  0.7 3.1 %copy-start.6 = (bf16[394,768]{1,0:T(8,128)(2,1)S(1)}, bf16[394,768]{1,0:T(8,128)(2,1)}, u32[]{:S(2)}) copy-start(bf16[394,768]{1,0:T(8,128)(2,1)} %param.16) | copy-start | bytes 1815556
  0.7 3.1 %copy-start.27 = (f32[768]{0:T(1024)S(1)}, f32[768]{0:T(1024)}, u32[]{:S(2)}) copy-start(f32[768]{0:T(1024)} %param.17) | copy-start | bytes 9220
  0.7 3.0 %copy-start.25 = (s32[394,2]{0,1:T(2,128)S(1)}, s32[394,2]{0,1:T(2,128)}, u32[]{:S(2)}) copy-start(s32[394,2]{0,1:T(2,128)} %param.29) | copy-start | bytes 9460
  0.7 3.0 %copy-start.34 = (f32[768]{0:T(1024)S(1)}, f32[768]{0:T(1024)}, u32[]{:S(2)}) copy-start(f32[768]{0:T(1024)} %param.18) | copy-start | bytes 9220
  0.7 3.0 %copy-start.30 = (s32[394,2]{0,1:T(2,128)S(1)}, s32[394,2]{0,1:T(2,128)}, u32[]{:S(2)}) copy-start(s32[394,2]{0,1:T(2,128)} %param.30) | copy-start | bytes 9460
  10.6 0.7 copy-start.12
  11.0 1.0 copy-start.8
  11.2 1.5 copy-start.20
  12.7 13.3 %copy-start.14 = (bf16[394,192]{0,1:T(8,128)(2,1)}, bf16[394,192]{0,1:T(8,128)(2,1)S(1)}, u32[]{:S(2)}) copy-start(bf16[394,192]{0,1:T(8,128)(2,1)S(1)} %reshape.255) | copy-start | bytes 453892
  12.7 12.9 %copy-start.24 = (f32[768]{0:T(1024)S(1)}, f32[768]{0:T(1024)}, u32[]{:S(2)}) copy-start(f32[768]{0:T(1024)} %param.21) | copy-start | bytes 9220
  25.7 0.7 copy-start.26
  25.7 0.7 copy-start.29
  26.4 0.7 copy-start.28
  26.4 1.3 copy-start.22
  27.7 1.3 copy-start.1
  27.7 1.6 copy-start.2
  27.7 1.6 copy-start.4
  27.7 1.6 copy-start.5
  88.3 1.4 copy-start.16
  103.0 1.8 copy-start.15
  104.8 1.1 copy-start.10
  104.8 1.2 copy-start.21
  106.4 1.8 copy-start.9
  108.2 0.9 copy-start.13
  110.5 1.7 copy-start.23
  110.5 1.8 copy-start.35
  112.3 2.0 %copy-start.19 = (bf16[768,192]{0,1:T(8,128)(2,1)S(1)}, bf16[768,192]{0,1:T(8,128)(2,1)}, u32[]{:S(2)}) copy-start(bf16[768,192]{0,1:T(8,128)(2,1)} %convolution_convert_fusion.5) | copy-start | bytes 884740
  115.2 1.1 copy-start.3
  116.3 50.5 %copy-start.7 = (bf16[394,768]{1,0:T(8,128)(2,1)S(1)}, bf16[394,768]{1,0:T(8,128)(2,1)}, u32[]{:S(2)}) copy-start(bf16[394,768]{1,0:T(8,128)(2,1)} %param.16) | copy-start | bytes 1815556
  116.3 51.0 %copy-start.11 = (f32[394,768]{1,0:T(8,128)S(1)}, f32[394,768]{1,0:T(8,128)}, u32[]{:S(2)}) copy-start(f32[394,768]{1,0:T(8,128)} %copy-done.10) | copy-start | bytes 3631108
  173.9 1.0 copy-start.18
  175.1 2.2 %copy-start.33 = (bf16[8,128,768]{2,1,0:T(8,128)(2,1)S(1)}, bf16[8,128,768]{2,1,0:T(8,128)(2,1)}, u32[]{:S(2)}) copy-start(bf16[8,128,768]{2,1,0:T(8,128)(2,1)} %get-tuple-element.36) | copy-start | bytes 4718596
  176.0 2.2 %copy-start.32 = (bf16[8,4,32,768]{3,2,1,0:T(8,128)(2,1)S(1)}, bf16[8,4,32,768]{3,2,1,0:T(8,128)(2,1)}, u32[]{:S(2)}) copy-start(bf16[8,4,32,768]{3,2,1,0:T(8,128)(2,1)} %get-tuple-element.35) | copy-start | bytes 4718596
  178.1 2.9 %copy-start.17 = (bf16[8,4,32,768]{3,2,1,0:T(8,128)(2,1)S(1)}, bf16[8,4,32,768]{3,2,1,0:T(8,128)(2,1)}, u32[]{:S(2)}) copy-start(bf16[8,4,32,768]{3,2,1,0:T(8,128)(2,1)} %get-tuple-element.39) | copy-start | bytes 4718596
  178.1 2.9 %copy-start.31 = (bf16[8,128,768]{2,1,0:T(8,128)(2,1)S(1)}, bf16[8,128,768]{2,1,0:T(8,128)(2,1)}, u32[]{:S(2)}) copy-start(bf16[8,128,768]{2,1,0:T(8,128)(2,1)} %get-tuple-element.38) | copy-start | bytes 4718596
